TPU v7x, 512 devices: a whole 4x8x8 slice. The times are simulated.
512 devices in a mesh: freq: 128 (over z, y, core), panel: 4 (over x).
Axes of the slice: x: 4, y: 8, z: 8, core: 2. Of those that a mesh axis runs over, the one named last changes fastest.
Arguments:
- wave: bfloat16 [2, 128, 1600, 1600], P(None, 'freq', 'panel'), may hold values from -0.15625 to 0.15625
- observed: float32 [4, 6400, 512], P('panel', 'freq'), may hold values from -25 to 25
Outputs:
- solution: float32 [25600, 512], P('freq')
All inputs are finite; a program needn't handle non-finite values.
Results may differ from a plain program's by a relative error of at most 0.0085.
Values may be sent and summed in bfloat16 or wider, within the bound.
A program may use at most 64 MiB of HBM per device.

v0:
```python
import math

import jax
import jax.numpy as jnp
from jax import lax
from jax.sharding import PartitionSpec as P

VS = 16
ITERS = 3


precise = lax.Precision.HIGHEST
epsilon = 1e-06


def transform_tables(freq_total, samples):
    freq_index = lax.broadcasted_iota(jnp.int32, (freq_total, samples), 0) + 1
    time_index = lax.broadcasted_iota(jnp.int32, (freq_total, samples), 1)
    phases = (freq_index * time_index % samples).astype(jnp.float32) * (2.0 * math.pi / samples)
    factor = math.sqrt(2.0 / samples)
    return jnp.stack([factor * jnp.cos(phases), -factor * jnp.sin(phases)])


def spectrum_flat(rows, table):
    return jnp.einsum("cft,rt->fcr", table, rows, precision=precise).reshape(-1)


def owner_layout(received, blocks, local_freqs):
    pieces = received.reshape(blocks, local_freqs, 2, -1).transpose(2, 1, 0, 3)
    return pieces.reshape(2, local_freqs, -1)


def trace_layout(spectrum, blocks):
    parts, local_freqs, total_rows = spectrum.shape
    pieces = spectrum.reshape(parts, local_freqs, blocks, total_rows // blocks).transpose(
        2, 1, 0, 3
    )
    return pieces.reshape(-1)


def time_traces(received, table, blocks, local_freqs):
    pieces = received.reshape(blocks, local_freqs, 2, -1).astype(jnp.float32)
    folded = table.reshape(2, blocks, local_freqs, table.shape[2])
    return jnp.einsum("jlcr,cjlt->rt", pieces, folded, precision=precise)


def forward_product(spectrum, wave):

    def product_of(left, right):
        return jnp.einsum("fvs,frs->fvr", left, right, preferred_element_type=jnp.float32)

    real_out = product_of(spectrum[0], wave[0]) - product_of(spectrum[1], wave[1])
    imag_out = product_of(spectrum[0], wave[1]) + product_of(spectrum[1], wave[0])
    return jnp.stack([real_out, imag_out]).astype(jnp.bfloat16)


def adjoint_product(spectrum, wave):

    def product_of(left, right):
        return jnp.einsum("fvr,frs->fvs", left, right, preferred_element_type=jnp.float32)

    real_out = product_of(spectrum[0], wave[0]) + product_of(spectrum[1], wave[1])
    imag_out = product_of(spectrum[1], wave[0]) - product_of(spectrum[0], wave[1])
    return jnp.stack([real_out, imag_out])


def on_device(wave, observed):
    local_freqs = wave.shape[1]
    panel_rows = wave.shape[2]
    blocks = lax.axis_size("freq")
    freq_total = local_freqs * blocks
    samples = observed.shape[2]
    table = transform_tables(freq_total, samples)

    def summed_panels(partial_sum):
        return lax.psum(partial_sum, "panel")

    def adjoint(data):
        lines = spectrum_flat(data, table).astype(jnp.bfloat16)
        moved_in = lax.all_to_all(lines, "freq", split_axis=0, concat_axis=0, tiled=True)
        spectrum = owner_layout(moved_in, blocks, local_freqs).reshape(
            2, local_freqs, VS, panel_rows
        )
        partial_sum = adjoint_product(spectrum, wave)
        total = summed_panels(partial_sum).reshape(2, local_freqs, -1)
        moved = lax.all_to_all(
            trace_layout(total, blocks), "freq", split_axis=0, concat_axis=0, tiled=True
        )
        return time_traces(moved, table, blocks, local_freqs)

    def data_norm(field):
        return jnp.sqrt(lax.psum(jnp.sum(field * field), ("freq", "panel")) + epsilon)

    def model_norm(field):
        return jnp.sqrt(lax.psum(jnp.sum(field * field), "freq") + epsilon)

    data_vector = observed[0]
    beta = data_norm(data_vector)
    data_vector = data_vector / beta
    model_vector = adjoint(data_vector)
    alpha = model_norm(model_vector)
    model_vector = model_vector / alpha
    direction = model_vector
    solution = jnp.zeros_like(model_vector)
    phi_bar = beta
    rho_bar = alpha
    for step in range(ITERS):
        forward_lines = spectrum_flat(model_vector, table).astype(jnp.bfloat16)
        forward_moved_in = lax.all_to_all(
            forward_lines, "freq", split_axis=0, concat_axis=0, tiled=True
        )
        forward_spectrum = owner_layout(forward_moved_in, blocks, local_freqs).reshape(
            2, local_freqs, VS, -1
        )
        product = forward_product(forward_spectrum, wave).reshape(2, local_freqs, -1)
        forward_moved = lax.all_to_all(
            trace_layout(product, blocks), "freq", split_axis=0, concat_axis=0, tiled=True
        )
        data_vector = time_traces(forward_moved, table, blocks, local_freqs) - alpha * data_vector
        beta = data_norm(data_vector)
        data_vector = data_vector / beta
        model_vector = adjoint(data_vector) - beta * model_vector
        alpha = model_norm(model_vector)
        model_vector = model_vector / alpha
        rho_new = jnp.sqrt(rho_bar * rho_bar + beta * beta)
        cosine = rho_bar / rho_new
        sine_part = beta / rho_new
        theta = sine_part * alpha
        rho_bar = -cosine * alpha
        phi_value = cosine * phi_bar
        phi_bar = sine_part * phi_bar
        solution = solution + phi_value / rho_new * direction
        direction = model_vector - theta / rho_new * direction
    return solution


def solution(mesh):
    placed = (P(None, "freq", "panel", None), P("panel", "freq", None))
    return jax.shard_map(
        on_device, mesh=mesh, in_specs=placed, out_specs=P("freq", None), check_vma=False
    )
```

profile of v0, /device:TPU:1, one launch (start us, length us, event | category | flops | bytes accessed | tf_op | source)
XLA Modules:
  0.0 1600.5 jit_solution(7903671710847964002)
XLA Ops:
  6.5 1.9 multiply_reduce_fusion.5
  8.4 106.0 %psum.70 = f32[]{:T(128)} all-reduce(f32[]{:T(128)} %multiply_reduce_fusion.5), channel_id=1, replica_groups=mesh['freq'=128,'panel'=4] {'freq','panel'}, use_global_device_ids=true, to_apply=%region_1.2 | all-reduce | flops 1 | bytes 8 | tf_op jit(solution)/shard_map/psum | solution.py:92
  118.6 20.5 %all_to_all.90 = bf16[128,100,1]{1,2,0:T(2,128)(2,1)S(1)} all-to-all(bf16[128,100,1]{1,2,0:T(2,128)(2,1)S(1)} %copy.37), channel_id=1, replica_groups=mesh['freq'=128,'panel'=4] {'freq'}, dimensions={0} | all-to-all | bytes 51200 | tf_op jit(solution)/shard_map/all_to_all | solution.py:80
  143.3 40.2 %all-reduce.4.cloned.1.call-done = f32[128,400,1]{0,1,2:T(8,128)} async-done(((f32[128,400,1]{0,1,2:T(8,128)}), f32[128,400,1]{0,1,2:T(8,128)}) %all-reduce.4.cloned.1.call-update) | async-done | bytes 204816 | tf_op jit(solution)/shard_map/psum | solution.py:76
  184.6 31.3 %all_to_all.91 = f32[128,400,1]{1,2,0:T(1,128)S(1)} all-to-all(f32[128,400,1]{1,2,0:T(1,128)S(1)} %copy.42), channel_id=1, replica_groups=mesh['freq'=128,'panel'=4] {'freq'}, dimensions={0} | all-to-all | bytes 409600 | tf_op jit(solution)/shard_map/all_to_all | solution.py:86
  216.0 2.2 multiply_reduce_fusion.2
  218.3 247.2 %psum.72 = f32[]{:T(128)} all-reduce(f32[]{:T(128)} %get-tuple-element.19), channel_id=1, replica_groups=mesh['freq'=128,'panel'=4] {'freq'}, use_global_device_ids=true, to_apply=%region_4.5 | all-reduce | flops 1 | bytes 8 | tf_op jit(solution)/shard_map/psum | solution.py:95
  470.3 19.2 %all_to_all.92 = bf16[128,2,200]{2,1,0:T(2,128)(2,1)S(1)} all-to-all(bf16[128,2,200]{2,1,0:T(2,128)(2,1)S(1)} %reshape.643), channel_id=1, replica_groups=mesh['freq'=128,'panel'=4] {'freq'}, dimensions={0} | all-to-all | bytes 204800 | tf_op jit(solution)/shard_map/all_to_all | solution.py:109
  494.5 16.5 %all_to_all.93 = bf16[128,100,1]{1,2,0:T(2,128)(2,1)S(1)} all-to-all(bf16[128,100,1]{1,2,0:T(2,128)(2,1)S(1)} %reshape.640), channel_id=1, replica_groups=mesh['freq'=128,'panel'=4] {'freq'}, dimensions={0} | all-to-all | bytes 51200 | tf_op jit(solution)/shard_map/all_to_all | solution.py:116
  511.2 1.9 multiply_reduce_fusion.4
  513.1 94.5 %psum.73 = f32[]{:T(128)} all-reduce(f32[]{:T(128)} %get-tuple-element.21), channel_id=1, replica_groups=mesh['freq'=128,'panel'=4] {'freq','panel'}, use_global_device_ids=true, to_apply=%region_6.7 | all-reduce | flops 1 | bytes 8 | tf_op jit(solution)/shard_map/psum | solution.py:92
  610.1 19.3 %all_to_all.94 = bf16[128,100,1]{1,2,0:T(2,128)(2,1)S(1)} all-to-all(bf16[128,100,1]{1,2,0:T(2,128)(2,1)S(1)} %copy.53), channel_id=1, replica_groups=mesh['freq'=128,'panel'=4] {'freq'}, dimensions={0} | all-to-all | bytes 51200 | tf_op jit(solution)/shard_map/all_to_all | solution.py:80
  632.3 40.8 %all-reduce.6.cloned.1.call-done = f32[128,400,1]{0,1,2:T(8,128)} async-done(((f32[128,400,1]{0,1,2:T(8,128)}), f32[128,400,1]{0,1,2:T(8,128)}) %all-reduce.6.cloned.1.call-update) | async-done | bytes 204816 | tf_op jit(solution)/shard_map/psum | solution.py:76
  674.2 31.4 %all_to_all.95 = f32[128,400,1]{1,2,0:T(1,128)} all-to-all(f32[128,400,1]{1,2,0:T(1,128)S(1)} %copy.58), channel_id=1, replica_groups=mesh['freq'=128,'panel'=4] {'freq'}, dimensions={0} | all-to-all | bytes 409600 | tf_op jit(solution)/shard_map/all_to_all | solution.py:86
  706.7 2.9 multiply_reduce_fusion.1
  709.7 247.2 %psum.75 = f32[]{:T(128)} all-reduce(f32[]{:T(128)} %get-tuple-element.23), channel_id=1, replica_groups=mesh['freq'=128,'panel'=4] {'freq'}, use_global_device_ids=true, to_apply=%region_9.10 | all-reduce | flops 1 | bytes 8 | tf_op jit(solution)/shard_map/psum | solution.py:95
  957.6 1.8 convolution_convert_fusion.1
  961.2 19.2 %all_to_all.96 = bf16[128,2,200]{2,1,0:T(2,128)(2,1)S(1)} all-to-all(bf16[128,2,200]{2,1,0:T(2,128)(2,1)S(1)} %reshape.645), channel_id=1, replica_groups=mesh['freq'=128,'panel'=4] {'freq'}, dimensions={0} | all-to-all | bytes 204800 | tf_op jit(solution)/shard_map/all_to_all | solution.py:109
  985.5 16.5 %all_to_all.97 = bf16[128,100,1]{1,2,0:T(2,128)(2,1)S(1)} all-to-all(bf16[128,100,1]{1,2,0:T(2,128)(2,1)S(1)} %reshape.641), channel_id=1, replica_groups=mesh['freq'=128,'panel'=4] {'freq'}, dimensions={0} | all-to-all | bytes 51200 | tf_op jit(solution)/shard_map/all_to_all | solution.py:116
  1002.1 1.9 multiply_reduce_fusion.3
  1004.1 94.5 %psum.76 = f32[]{:T(128)} all-reduce(f32[]{:T(128)} %get-tuple-element.25), channel_id=1, replica_groups=mesh['freq'=128,'panel'=4] {'freq','panel'}, use_global_device_ids=true, to_apply=%region_11.12 | all-reduce | flops 1 | bytes 8 | tf_op jit(solution)/shard_map/psum | solution.py:92
  1101.0 19.3 %all_to_all.98 = bf16[128,100,1]{1,2,0:T(2,128)(2,1)S(1)} all-to-all(bf16[128,100,1]{1,2,0:T(2,128)(2,1)S(1)} %copy.69), channel_id=1, replica_groups=mesh['freq'=128,'panel'=4] {'freq'}, dimensions={0} | all-to-all | bytes 51200 | tf_op jit(solution)/shard_map/all_to_all | solution.py:80
  1123.1 40.9 %all-reduce.8.cloned.1.call-done = f32[128,400,1]{0,1,2:T(8,128)} async-done(((f32[128,400,1]{0,1,2:T(8,128)}), f32[128,400,1]{0,1,2:T(8,128)}) %all-reduce.8.cloned.1.call-update) | async-done | bytes 204816 | tf_op jit(solution)/shard_map/psum | solution.py:76
  1165.1 31.6 %all_to_all.99 = f32[128,400,1]{1,2,0:T(1,128)} all-to-all(f32[128,400,1]{1,2,0:T(1,128)S(1)} %copy.74), channel_id=1, replica_groups=mesh['freq'=128,'panel'=4] {'freq'}, dimensions={0} | all-to-all | bytes 409600 | tf_op jit(solution)/shard_map/all_to_all | solution.py:86
  1197.9 3.1 multiply_reduce_fusion
  1201.0 247.0 %psum.78 = f32[]{:T(128)} all-reduce(f32[]{:T(128)} %get-tuple-element.27), channel_id=1, replica_groups=mesh['freq'=128,'panel'=4] {'freq'}, use_global_device_ids=true, to_apply=%region_14.15 | all-reduce | flops 1 | bytes 8 | tf_op jit(solution)/shard_map/psum | solution.py:95
  1452.3 19.2 %all_to_all.100 = bf16[128,2,200]{2,1,0:T(2,128)(2,1)S(1)} all-to-all(bf16[128,2,200]{2,1,0:T(2,128)(2,1)S(1)} %reshape.647), channel_id=1, replica_groups=mesh['freq'=128,'panel'=4] {'freq'}, dimensions={0} | all-to-all | bytes 204800 | tf_op jit(solution)/shard_map/all_to_all | solution.py:109
  1477.2 5.5 all-to-all-start.11
  1483.1 11.1 all-to-all-done.11
  1494.4 2.0 fusion.93
  1496.4 94.5 %psum.79 = f32[]{:T(128)} all-reduce(f32[]{:T(128)} %fusion.93), channel_id=1, replica_groups=mesh['freq'=128,'panel'=4] {'freq','panel'}, use_global_device_ids=true, to_apply=%region_16.17 | all-reduce | flops 1 | bytes 8 | tf_op jit(solution)/shard_map/psum | solution.py:92
  1591.7 2.1 multiply_add_fusion
  (157 shorter events, 47.6 us)
Async XLA Ops:
  6.5 134.8 %copy-start = (bf16[2,1,400,1600]{3,2,1,0:T(8,128)(2,1)S(1)}, bf16[2,1,400,1600]{3,2,1,0:T(8,128)(2,1)}, u32[]{:S(2)}) copy-start(bf16[2,1,400,1600]{3,2,1,0:T(8,128)(2,1)} %param.2) | copy-start | bytes 7680004
  6.5 177.0 %all-reduce.4.cloned.1.call-start = ((), (), s32[]{:S(2)}) async-start(), calls=%async_computation.12 | async-start | bytes 409600 | tf_op jit(solution)/shard_map/psum | solution.py:76
  116.3 0.7 copy-start.7
  116.3 25.6 %copy-start.1 = (f32[1,128,512]{2,1,0:T(8,128)}, f32[1,128,512]{2,1,0:T(8,128)S(1)}, u32[]{:S(2)}) copy-start(f32[1,128,512]{2,1,0:T(8,128)S(1)} %get-tuple-element.17) | copy-start | bytes 786436
  143.3 529.8 %all-reduce.6.cloned.1.call-start = ((), (), s32[]{:S(2)}) async-start(), calls=%async_computation.13 | async-start | bytes 409600 | tf_op jit(solution)/shard_map/psum | solution.py:76
  491.2 20.0 %copy-start.2 = (f32[1,128,512]{2,1,0:T(8,128)S(1)}, f32[1,128,512]{2,1,0:T(8,128)}, u32[]{:S(2)}) copy-start(f32[1,128,512]{2,1,0:T(8,128)} %copy-done.1) | copy-start | bytes 786436
  513.1 117.7 %copy-start.9 = (f32[50,512]{1,0:T(8,128)}, f32[50,512]{1,0:T(8,128)S(1)}, u32[]{:S(2)}) copy-start(f32[50,512]{1,0:T(8,128)S(1)} %get-tuple-element.22) | copy-start | bytes 307204
  632.2 531.8 %all-reduce.8.cloned.1.call-start = ((), (), s32[]{:S(2)}) async-start(), calls=%async_computation.14 | async-start | bytes 409600 | tf_op jit(solution)/shard_map/psum | solution.py:76
  705.6 252.0 %copy-start.3 = (f32[1,128,512]{2,1,0:T(8,128)S(1)}, f32[1,128,512]{2,1,0:T(8,128)}, u32[]{:S(2)}) copy-start(f32[1,128,512]{2,1,0:T(8,128)} %copy-done.1) | copy-start | bytes 786436
  982.1 20.0 %copy-start.4 = (f32[1,128,512]{2,1,0:T(8,128)S(1)}, f32[1,128,512]{2,1,0:T(8,128)}, u32[]{:S(2)}) copy-start(f32[1,128,512]{2,1,0:T(8,128)} %copy-done.1) | copy-start | bytes 786436
  1004.1 117.7 %copy-start.8 = (f32[50,512]{1,0:T(8,128)}, f32[50,512]{1,0:T(8,128)S(1)}, u32[]{:S(2)}) copy-start(f32[50,512]{1,0:T(8,128)S(1)} %get-tuple-element.26) | copy-start | bytes 307204
  1196.8 251.9 %copy-start.5 = (f32[1,128,512]{2,1,0:T(8,128)S(1)}, f32[1,128,512]{2,1,0:T(8,128)}, u32[]{:S(2)}) copy-start(f32[1,128,512]{2,1,0:T(8,128)} %copy-done.1) | copy-start | bytes 786436
  1473.2 21.2 %copy-start.6 = (f32[1,128,512]{2,1,0:T(8,128)S(1)}, f32[1,128,512]{2,1,0:T(8,128)}, u32[]{:S(2)}) copy-start(f32[1,128,512]{2,1,0:T(8,128)} %copy-done.1) | copy-start | bytes 786436
  1477.2 17.1 %all-to-all-start.11 = ((bf16[128,100,1]{1,2,0:T(2,128)(2,1)}), bf16[128,100,1]{1,2,0:T(2,128)(2,1)S(1)}, u32[]{:S(2)}, u32[]{:S(2)}) async-start(bf16[128,100,1]{1,2,0:T(2,128)(2,1)} %reshape.642), calls=%async_computation.11 | async-start | bytes 131072 | tf_op jit(solution)/shard_map/all_to_all | solution.py:116
Sparse Core Ops, SparseCore 0:
  143.4 40.0 all-reduce.3
  632.4 40.7 all-reduce.5
  1123.3 40.7 all-reduce.7
where the time goes:
time: 1610 us; the launch traced here: 1600 us
  blocking collectives  1380 us (86%)
  waiting for transfers between devices  133 us (8%)
  matrix products  34.4 us (2%)
  local copies, waits for them, and re-layouts  23 us (1%)
  between operations  19.3 us (1%)
    psum x3, blocking collectives, model_norm(): return jnp.sqrt(lax.psum(jnp.sum(field * field), 'freq') + epsilon)  741 us
    psum x4, blocking collectives, data_norm(): lax.psum(jnp.sum(field * field), ('freq', 'panel')) + epsilon  390 us
    psum x3, waiting for transfers between devices, summed_panels(): return lax.psum(partial_sum, 'panel')  122 us
    all_to_all x3, blocking collectives, adjoint(): lax.all_to_all(trace_layout(total, blocks), 'freq', split_axis=0, concat_...  94.4 us
    all_to_all x3, blocking collectives, adjoint(): lax.all_to_all(lines, 'freq', split_axis=0, concat_axis=0, tiled=True)  59.1 us
    all_to_all x3, blocking collectives, on_device(): lax.all_to_all(forward_lines, 'freq', split_axis=0, concat_axis=0, tiled=...  57.7 us
    all_to_all x2, blocking collectives, on_device(): lax.all_to_all(trace_layout(product, blocks), 'freq', split_axis=0, conca...  33 us
  transfers between devices with their start and end apart: 4, of which 4 were waited for; matrix products, arithmetic and copies ran while one was open for 0% of the time, Pallas kernels for 0%

commit v1 on v0

v1 whole, which is shorter than its diff:
```python
import math

import jax
import jax.numpy as jnp
from jax import lax
from jax.sharding import PartitionSpec as P

VS = 16
ITERS = 3
SCALE = 0.5

precise = lax.Precision.HIGHEST
epsilon = 1e-06


def transform_tables(freq_total, samples):
    freq_index = lax.broadcasted_iota(jnp.int32, (freq_total, samples), 0) + 1
    time_index = lax.broadcasted_iota(jnp.int32, (freq_total, samples), 1)
    phases = (freq_index * time_index % samples).astype(jnp.float32) * (2.0 * math.pi / samples)
    factor = math.sqrt(2.0 / samples)
    return jnp.stack([factor * jnp.cos(phases), -factor * jnp.sin(phases)])


def two_parts(field):
    high = lax.reduce_precision(field, 8, 7)
    return jnp.concatenate([high, field - high]).astype(jnp.bfloat16)


def forward_product(model, wave):
    rows = two_parts(model.reshape(2 * VS, -1))

    def product_of(right):
        both = lax.dot_general(
            rows, right, (((1,), (1,)), ((), ())), preferred_element_type=jnp.float32
        )
        return both[: 2 * VS] + both[2 * VS :]

    by_real, by_imag = product_of(wave[0]), product_of(wave[1])
    return SCALE * jnp.stack([by_real[:VS] - by_imag[VS:], by_imag[:VS] + by_real[VS:]])


def adjoint_product(rows, wave):

    def product_of(right):
        both = jnp.dot(rows, right, preferred_element_type=jnp.float32)
        return both if rows.shape[0] == 2 * VS else both[: 2 * VS] + both[2 * VS :]

    by_real, by_imag = product_of(wave[0]), product_of(wave[1])
    return SCALE * jnp.stack([by_real[:VS] + by_imag[VS:], by_real[VS:] - by_imag[:VS]])


def iterate_weights(data_square, moments):
    model_norms = [jnp.sqrt(moments[2 * k]) for k in range(ITERS)]
    data_norms = [jnp.sqrt(data_square)] + [jnp.sqrt(moments[2 * k + 1]) for k in range(ITERS)]

    def ratio(top, bottom):
        return jnp.where(bottom > 0, top / jnp.where(bottom > 0, bottom, 1.0), 0.0)

    model_gram = [
        [ratio(ratio(moments[i + j], model_norms[i]), model_norms[j]) for j in range(ITERS)]
        for i in range(ITERS)
    ]

    def data_inner(i, j):
        low, high = min(i, j), max(i, j)
        if high == 0:
            return data_square
        if low == 0:
            return moments[high - 1]
        return moments[low + high - 1]

    data_gram = [
        [ratio(ratio(data_inner(i, j), data_norms[i]), data_norms[j]) for j in range(ITERS + 1)]
        for i in range(ITERS + 1)
    ]

    def norm_of(weights, gram):
        total = 0.0
        for i in range(len(weights)):
            total += weights[i] * weights[i] * ratio(gram[i][i], gram[i][i])
            for j in range(i):
                total += 2.0 * weights[i] * weights[j] * gram[i][j]
        return jnp.sqrt(jnp.maximum(total, 0.0) + epsilon)

    up = [ratio(data_norms[k + 1], model_norms[k]) / SCALE for k in range(ITERS)]
    down = [ratio(model_norms[k], data_norms[k]) / SCALE for k in range(ITERS)]
    zero = jnp.zeros_like(data_square)
    beta = jnp.sqrt(data_square + epsilon)
    data_vector = [data_norms[0] / beta] + [zero] * ITERS
    model_vector = [data_vector[k] * down[k] for k in range(ITERS)]
    alpha = norm_of(model_vector, model_gram)
    model_vector = [weight / alpha for weight in model_vector]
    direction = model_vector
    solution = [zero] * ITERS
    phi_bar = beta
    rho_bar = alpha
    for step in range(ITERS):
        image = [zero] + [model_vector[k] * up[k] for k in range(ITERS)]
        data_vector = [new - alpha * old for new, old in zip(image, data_vector)]
        beta = norm_of(data_vector, data_gram)
        data_vector = [weight / beta for weight in data_vector]
        rho_new = jnp.sqrt(rho_bar * rho_bar + beta * beta)
        cosine = rho_bar / rho_new
        sine_part = beta / rho_new
        phi_value = cosine * phi_bar
        phi_bar = sine_part * phi_bar
        solution = [
            old + phi_value / rho_new * weight for old, weight in zip(solution, direction)
        ]
        if step < ITERS - 1:
            image = [data_vector[k] * down[k] for k in range(ITERS)]
            model_vector = [new - beta * old for new, old in zip(image, model_vector)]
            alpha = norm_of(model_vector, model_gram)
            model_vector = [weight / alpha for weight in model_vector]
            theta = sine_part * alpha
            rho_bar = -cosine * alpha
            direction = [
                weight - theta / rho_new * old for weight, old in zip(model_vector, direction)
            ]
    return [ratio(weight, norm) for weight, norm in zip(solution, model_norms)]


def on_device(wave, observed):
    wave = wave[:, 0]
    panel_rows, sources = wave.shape[1:]
    blocks = lax.axis_size("freq")
    panels = lax.axis_size("panel")
    samples = observed.shape[2]
    table = transform_tables(blocks, samples)
    data = observed[0]

    def exchange(lines):
        return lax.all_to_all(lines, "freq", split_axis=0, concat_axis=0, tiled=True)

    lines = jnp.einsum("cft,rt->fcr", table, data, precision=precise).astype(jnp.bfloat16)
    moved_in = exchange(lines.reshape(-1)).reshape(blocks, 2, -1)
    rows = moved_in.transpose(1, 0, 2).reshape(2 * VS, panel_rows)

    bases, squares = [], [jnp.sum(data * data)]
    for step in range(ITERS):
        model = lax.psum(adjoint_product(rows, wave), "panel")
        image = forward_product(model, wave)
        bases.append(model)
        squares += [jnp.sum(model * model) / panels, jnp.sum(image * image)]
        rows = two_parts(image.reshape(2 * VS, -1))
    squares = lax.psum(jnp.stack(squares), ("freq", "panel"))
    weights = iterate_weights(squares[0], [squares[1 + k] for k in range(2 * ITERS)])
    spectrum = sum(weight * basis for weight, basis in zip(weights, bases))
    spectrum = spectrum.astype(jnp.bfloat16).reshape(2, blocks, -1)
    moved = exchange(spectrum.transpose(1, 0, 2).reshape(-1)).reshape(blocks, 2, -1)
    return jnp.einsum("jcr,cjt->rt", moved.astype(jnp.float32), table, precision=precise)


def solution(mesh):
    placed = (P(None, "freq", "panel", None), P("panel", "freq", None))
    return jax.shard_map(
        on_device, mesh=mesh, in_specs=placed, out_specs=P("freq", None), check_vma=False
    )
```

time: 1610 us -> 359 us (0.22)
  blocking collectives: 1380 us -> 152 us
  matrix products: 34.4 us -> 9.22 us
  local copies, waits for them, and re-layouts: 23 us -> 5.31 us
    psum x7 -> x1, blocking collectives: 1130 us -> 99.4 us  [on_device(): squares = lax.psum(jnp.stack(squares), ('freq', 'panel'))]
    all_to_all x11 -> x2, blocking collectives: 244 us -> 52.3 us  [exchange(): lax.all_to_all(lines, 'freq', split_axis=0, concat_axis=0, tiled=True)]
    dot_general x36 -> x14, matrix products: 34.4 us -> 9.22 us  [the longest x6 3.43 us: product_of(): both = jnp.dot(rows, right, preferred_element_type=jnp.float32)]
    psum x3, waiting for transfers between devices: 122 us -> 143 us  [on_device(): model = lax.psum(adjoint_product(rows, wave), 'panel')]
  transfers between devices with their start and end apart: 4 -> 3, of which waited for: 4 -> 3; matrix products, arithmetic and copies ran while one was open for 0% -> 1% of each run, Pallas kernels for 0% -> 0%
where the time goes in v1:
time: 359 us; the launch traced here: 358 us
  blocking collectives  152 us (42%)
  waiting for transfers between devices  143 us (40%)
  between operations  34.6 us (10%)
  other arithmetic  14.6 us (4%)
  matrix products  9.22 us (3%)
  local copies, waits for them, and re-layouts  5.31 us (1%)
    psum x3, waiting for transfers between devices, on_device(): model = lax.psum(adjoint_product(rows, wave), 'panel')  143 us
    psum x1, blocking collectives, on_device(): squares = lax.psum(jnp.stack(squares), ('freq', 'panel'))  99.4 us
    all_to_all x2, blocking collectives, exchange(): lax.all_to_all(lines, 'freq', split_axis=0, concat_axis=0, tiled=True)  52.3 us
  transfers between devices with their start and end apart: 3, of which 3 were waited for; matrix products, arithmetic and copies ran while one was open for 1% of the time, Pallas kernels for 0%

profile of v1, /device:TPU:1, one launch (start us, length us, event | category | flops | bytes accessed | tf_op | source)
XLA Modules:
  0.0 358.5 jit_solution(4462551454970142538)
XLA Ops:
  6.5 1.1 cosine_multiply_fusion
  7.7 1.5 fusion.24
  9.3 29.7 %all_to_all.18 = bf16[128,100,1]{1,2,0:T(2,128)(2,1)S(1)} all-to-all(bf16[128,100,1]{1,2,0:T(2,128)(2,1)S(1)} %copy.5), channel_id=1, replica_groups=mesh['freq'=128,'panel'=4] {'freq'}, dimensions={0} | all-to-all | bytes 51200 | tf_op jit(solution)/shard_map/all_to_all | solution.py:133
  39.4 1.7 fusion.10
  41.5 0.7 maximum_multiply_fusion
  42.3 42.4 %all-reduce.4.cloned.1.call-done = f32[2,16,1600]{2,1,0:T(8,128)} async-done(((f32[2,16,1600]{2,1,0:T(8,128)}), f32[2,16,1600]{2,1,0:T(8,128)}) %all-reduce.4.cloned.1.call-update) | async-done | bytes 204816 | tf_op jit(solution)/shard_map/psum | solution.py:141
  84.6 1.0 reduce-precision_convert_fusion.2
  85.6 0.5 fusion.20
  86.1 0.5 fusion.8
  86.7 0.6 multiply_reduce_fusion.4
  88.1 0.7 maximum_multiply_fusion.1
  88.9 0.7 fusion.47
  89.6 51.8 %all-reduce.6.cloned.1.call-done = f32[2,16,1600]{2,1,0:T(8,128)} async-done(((f32[2,16,1600]{2,1,0:T(8,128)}), f32[2,16,1600]{2,1,0:T(8,128)}) %all-reduce.6.cloned.1.call-update) | async-done | bytes 204816 | tf_op jit(solution)/shard_map/psum | solution.py:141
  141.4 1.0 reduce-precision_convert_fusion.1
  142.3 0.5 fusion.16
  142.9 0.5 fusion.4
  143.5 0.6 multiply_reduce_fusion.3
  144.9 0.7 maximum_multiply_fusion.2
  145.7 0.7 multiply_reduce_fusion.2
  146.9 1.7 multiply_reduce_fusion.1
  149.2 48.9 %all-reduce.8.cloned.1.call-done = f32[2,16,1600]{2,1,0:T(8,128)} async-done(((f32[2,16,1600]{2,1,0:T(8,128)}), f32[2,16,1600]{2,1,0:T(8,128)}) %all-reduce.8.cloned.1.call-update) | async-done | bytes 204816 | tf_op jit(solution)/shard_map/psum | solution.py:141
  198.1 1.0 reduce-precision_convert_fusion
  199.2 0.5 fusion.12
  200.3 0.7 multiply_reduce_fusion
  201.6 0.7 fusion.58
  202.3 2.6 stack.109
  204.9 99.4 %psum.31 = f32[7]{0:T(128)S(1)} all-reduce(f32[7]{0:T(128)S(1)} %stack.109), channel_id=1, replica_groups=mesh['freq'=128,'panel'=4] {'freq','panel'}, use_global_device_ids=true, to_apply=%region_10.11 | all-reduce | flops 7 | bytes 56 | tf_op jit(solution)/shard_map/psum | solution.py:146
  304.2 0.7 fusion.77
  324.2 1.1 add_convert_fusion
  326.3 1.4 reduce
  327.9 22.6 %all_to_all.19 = bf16[128,2,200]{2,1,0:T(2,128)(2,1)S(1)} all-to-all(bf16[128,2,200]{2,1,0:T(2,128)(2,1)S(1)} %reshape.144), channel_id=1, replica_groups=mesh['freq'=128,'panel'=4] {'freq'}, dimensions={0} | all-to-all | bytes 204800 | tf_op jit(solution)/shard_map/all_to_all | solution.py:133
  350.8 1.2 convolution_bitcast_fusion
  (51 shorter events, 4.8 us)
Async XLA Ops:
  6.5 34.5 %copy-start = (bf16[2,1,400,1600]{3,2,1,0:T(8,128)(2,1)S(1)}, bf16[2,1,400,1600]{3,2,1,0:T(8,128)(2,1)}, u32[]{:S(2)}) copy-start(bf16[2,1,400,1600]{3,2,1,0:T(8,128)(2,1)} %param.2) | copy-start | bytes 7680004
  6.5 78.1 %all-reduce.4.cloned.1.call-start = ((), (), s32[]{:S(2)}) async-start(), calls=%async_computation.2 | async-start | bytes 425984 | tf_op jit(solution)/shard_map/psum | solution.py:141
  42.2 99.2 %all-reduce.6.cloned.1.call-start = ((), (), s32[]{:S(2)}) async-start(), calls=%async_computation.3 | async-start | bytes 425984 | tf_op jit(solution)/shard_map/psum | solution.py:141
  87.3 1.6 copy-start.3
  88.9 109.3 %all-reduce.8.cloned.1.call-start = ((), (), s32[]{:S(2)}) async-start(), calls=%async_computation.4 | async-start | bytes 425984 | tf_op jit(solution)/shard_map/psum | solution.py:141
  144.1 1.6 copy-start.1
  198.1 2.1 copy-start.2
Sparse Core Ops, SparseCore 0:
  42.3 42.2 all-reduce.3
  89.0 52.3 all-reduce.5
  145.8 52.3 all-reduce.7

commit v2 on v1

--- a/solution.py
+++ b/solution.py
@@ -1,13 +1,19 @@
+import functools
 import math
 
 import jax
 import jax.numpy as jnp
 from jax import lax
+from jax.experimental import pallas as pl
+from jax.experimental.pallas import tpu as pltpu
 from jax.sharding import PartitionSpec as P
 
 VS = 16
 ITERS = 3
 SCALE = 0.5
+NEAR = 16
+GROUP = 8
+MESH = pl.DeviceIdType.MESH
 
 precise = lax.Precision.HIGHEST
 epsilon = 1e-06
@@ -22,31 +28,16 @@
 
 
 def two_parts(field):
-    high = lax.reduce_precision(field, 8, 7)
-    return jnp.concatenate([high, field - high]).astype(jnp.bfloat16)
-
-
-def forward_product(model, wave):
-    rows = two_parts(model.reshape(2 * VS, -1))
-
-    def product_of(right):
-        both = lax.dot_general(
-            rows, right, (((1,), (1,)), ((), ())), preferred_element_type=jnp.float32
-        )
-        return both[: 2 * VS] + both[2 * VS :]
-
-    by_real, by_imag = product_of(wave[0]), product_of(wave[1])
-    return SCALE * jnp.stack([by_real[:VS] - by_imag[VS:], by_imag[:VS] + by_real[VS:]])
-
-
-def adjoint_product(rows, wave):
-
-    def product_of(right):
-        both = jnp.dot(rows, right, preferred_element_type=jnp.float32)
-        return both if rows.shape[0] == 2 * VS else both[: 2 * VS] + both[2 * VS :]
-
-    by_real, by_imag = product_of(wave[0]), product_of(wave[1])
-    return SCALE * jnp.stack([by_real[:VS] + by_imag[VS:], by_real[VS:] - by_imag[:VS]])
+    high = field.astype(jnp.bfloat16)
+    low = (field - high.astype(jnp.float32)).astype(jnp.bfloat16)
+    return jnp.concatenate([high, low])
+
+
+def product_of(rows, right, side):
+    both = lax.dot_general(
+        rows, right, (((1,), (side,)), ((), ())), preferred_element_type=jnp.float32
+    )
+    return both if rows.shape[0] == 2 * VS else both[: 2 * VS] + both[2 * VS :]
 
 
 def iterate_weights(data_square, moments):
@@ -120,34 +111,191 @@
     return [ratio(weight, norm) for weight, norm in zip(solution, model_norms)]
 
 
+def square_of(field):
+    return jnp.broadcast_to(jnp.sum(field * field, keepdims=True), (1, 128))
+
+
+def lsqr_kernel(
+    panels,
+    blocks,
+    lines_ref,
+    wave_ref,
+    square_ref,
+    spectrum_ref,
+    parts,
+    arrived,
+    bases,
+    sums,
+    near,
+    far,
+    across,
+    part_send,
+    part_recv,
+    base_send,
+    base_recv,
+    near_send,
+    near_recv,
+    far_send,
+    far_recv,
+    across_send,
+    across_recv,
+):
+    me = lax.axis_index("panel")
+    freq = lax.axis_index("freq")
+    outer, inner = freq // NEAR, freq % NEAR
+    distant = blocks // NEAR
+
+    panel_peers = [{"panel": (me + k) % panels} for k in range(1, panels)]
+    near_peers = [{"freq": outer * NEAR + (inner + k) % NEAR} for k in range(1, NEAR)]
+    far_peers = [{"freq": (outer + k) % distant * NEAR + inner} for k in range(1, distant)]
+
+    barrier = pltpu.get_barrier_semaphore()
+    for peer in panel_peers + near_peers + far_peers:
+        pl.semaphore_signal(barrier, inc=1, device_id=peer, device_id_type=MESH)
+
+    sent = []
+
+    def copy_to(peer, source, target, send_sem, recv_sem):
+        copy = pltpu.make_async_remote_copy(
+            src_ref=source,
+            dst_ref=target,
+            send_sem=send_sem,
+            recv_sem=recv_sem,
+            device_id=peer,
+            device_id_type=MESH,
+        )
+        copy.start()
+        sent.append(copy)
+
+    def arrival(ref, recv_sem):
+        pltpu.make_async_copy(ref, ref, recv_sem).wait()
+
+    sums[...] = jnp.zeros_like(sums)
+    sums[0:1, :] = square_ref[...]
+    rows = lines_ref[...]
+    for step in range(ITERS):
+        by_real = product_of(rows, wave_ref[0], 0)
+        by_imag = product_of(rows, wave_ref[1], 0)
+        real_part = SCALE * (by_real[:VS] + by_imag[VS:])
+        imag_part = SCALE * (by_real[VS:] - by_imag[:VS])
+        parts[step, : panels // 2] = real_part.reshape(panels // 2, GROUP, -1)
+        parts[step, panels // 2 :] = imag_part.reshape(panels // 2, GROUP, -1)
+        if step == 0:
+            pl.semaphore_wait(barrier, len(panel_peers + near_peers + far_peers))
+        for k in range(1, panels):
+            copy_to(
+                panel_peers[k - 1],
+                parts.at[step, (me + k) % panels],
+                arrived.at[step, k - 1],
+                part_send.at[step, k - 1],
+                part_recv.at[step, k - 1],
+            )
+        total = parts[step, me]
+        for k in range(1, panels):
+            arrival(arrived.at[step, k - 1], part_recv.at[step, k - 1])
+            total = total + arrived[step, k - 1]
+        bases[step, me] = total
+        for k in range(1, panels):
+            copy_to(
+                panel_peers[k - 1],
+                bases.at[step, me],
+                bases.at[step, me],
+                base_send.at[step, k - 1],
+                base_recv.at[step, k - 1],
+            )
+        sums[2 * step + 1 : 2 * step + 2, :] = square_of(total)
+        for k in range(1, panels):
+            arrival(bases.at[step, (me + panels - k) % panels], base_recv.at[step, k - 1])
+        model_rows = two_parts(bases[step].reshape(2 * VS, -1))
+        by_real = product_of(model_rows, wave_ref[0], 1)
+        by_imag = product_of(model_rows, wave_ref[1], 1)
+        image = SCALE * jnp.concatenate(
+            [by_real[:VS] - by_imag[VS:], by_imag[:VS] + by_real[VS:]]
+        )
+        sums[2 * step + 2 : 2 * step + 3, :] = square_of(image)
+        if step < ITERS - 1:
+            rows = two_parts(image)
+
+    def summed(value, held, count, index, peers, send_sem, recv_sem):
+        held[index] = value
+        for k in range(1, count):
+            copy_to(
+                peers[k - 1],
+                held.at[index],
+                held.at[index],
+                send_sem.at[k - 1],
+                recv_sem.at[k - 1],
+            )
+        for k in range(1, count):
+            arrival(held.at[(index + count - k) % count], recv_sem.at[k - 1])
+        return jnp.sum(held[...], axis=0)
+
+    value = summed(sums[...], near, NEAR, inner, near_peers, near_send, near_recv)
+    value = summed(value, far, distant, outer, far_peers, far_send, far_recv)
+    value = summed(value, across, panels, me, panel_peers, across_send, across_recv)
+    squares = [value[k : k + 1, :] for k in range(2 * ITERS + 1)]
+    weights = iterate_weights(squares[0], squares[1:])
+    spectrum = sum(
+        weight[:, :1] * bases[step].reshape(2 * VS, -1) for step, weight in enumerate(weights)
+    )
+    spectrum_ref[...] = spectrum.astype(jnp.bfloat16)
+    for copy in sent:
+        copy.wait_send()
+
+
+def solved_spectrum(lines, wave, square, panels, blocks):
+    sources = wave.shape[2]
+    quarter = (GROUP, sources)
+    tile = (8, 128)
+    distant = blocks // NEAR
+    dma = pltpu.SemaphoreType.DMA
+    return pl.pallas_call(
+        functools.partial(lsqr_kernel, panels, blocks),
+        out_shape=jax.ShapeDtypeStruct((2 * VS, sources), jnp.bfloat16),
+        in_specs=[pl.BlockSpec(memory_space=pltpu.VMEM)] * 3,
+        out_specs=pl.BlockSpec(memory_space=pltpu.VMEM),
+        scratch_shapes=[
+            pltpu.VMEM((ITERS, panels, *quarter), jnp.float32),
+            pltpu.VMEM((ITERS, panels - 1, *quarter), jnp.float32),
+            pltpu.VMEM((ITERS, panels, *quarter), jnp.float32),
+            pltpu.VMEM(tile, jnp.float32),
+            pltpu.VMEM((NEAR, *tile), jnp.float32),
+            pltpu.VMEM((distant, *tile), jnp.float32),
+            pltpu.VMEM((panels, *tile), jnp.float32),
+            dma((ITERS, panels - 1)),
+            dma((ITERS, panels - 1)),
+            dma((ITERS, panels - 1)),
+            dma((ITERS, panels - 1)),
+            dma((NEAR - 1,)),
+            dma((NEAR - 1,)),
+            dma((distant - 1,)),
+            dma((distant - 1,)),
+            dma((panels - 1,)),
+            dma((panels - 1,)),
+        ],
+        compiler_params=pltpu.CompilerParams(
+            collective_id=0, has_side_effects=True, vmem_limit_bytes=32 * 1024 * 1024
+        ),
+    )(lines, wave, square)
+
+
 def on_device(wave, observed):
     wave = wave[:, 0]
-    panel_rows, sources = wave.shape[1:]
+    panel_rows = wave.shape[1]
     blocks = lax.axis_size("freq")
     panels = lax.axis_size("panel")
-    samples = observed.shape[2]
-    table = transform_tables(blocks, samples)
+    table = transform_tables(blocks, observed.shape[2])
     data = observed[0]
 
     def exchange(lines):
-        return lax.all_to_all(lines, "freq", split_axis=0, concat_axis=0, tiled=True)
+        moved = lax.all_to_all(lines.reshape(-1), "freq", split_axis=0, concat_axis=0, tiled=True)
+        return moved.reshape(blocks, 2, -1)
 
     lines = jnp.einsum("cft,rt->fcr", table, data, precision=precise).astype(jnp.bfloat16)
-    moved_in = exchange(lines.reshape(-1)).reshape(blocks, 2, -1)
-    rows = moved_in.transpose(1, 0, 2).reshape(2 * VS, panel_rows)
-
-    bases, squares = [], [jnp.sum(data * data)]
-    for step in range(ITERS):
-        model = lax.psum(adjoint_product(rows, wave), "panel")
-        image = forward_product(model, wave)
-        bases.append(model)
-        squares += [jnp.sum(model * model) / panels, jnp.sum(image * image)]
-        rows = two_parts(image.reshape(2 * VS, -1))
-    squares = lax.psum(jnp.stack(squares), ("freq", "panel"))
-    weights = iterate_weights(squares[0], [squares[1 + k] for k in range(2 * ITERS)])
-    spectrum = sum(weight * basis for weight, basis in zip(weights, bases))
-    spectrum = spectrum.astype(jnp.bfloat16).reshape(2, blocks, -1)
-    moved = exchange(spectrum.transpose(1, 0, 2).reshape(-1)).reshape(blocks, 2, -1)
+    rows = exchange(lines).transpose(1, 0, 2).reshape(2 * VS, panel_rows)
+    square = jnp.full((1, 128), jnp.sum(data * data))
+    spectrum = solved_spectrum(rows, wave, square, panels, blocks).reshape(2, blocks, -1)
+    moved = exchange(spectrum.transpose(1, 0, 2))
     return jnp.einsum("jcr,cjt->rt", moved.astype(jnp.float32), table, precision=precise)
 
 

time: 359 us -> 112 us (0.31)
  waiting for transfers between devices: 143 us -> 9.81 us
  blocking collectives: 152 us -> 22.8 us
  Pallas kernels: 0 us -> 48.9 us
  between operations: 34.6 us -> 0.11 us
  starting transfers between devices: 0.09 us -> 18.4 us
  other arithmetic: 14.6 us -> 4.21 us
  matrix products: 9.22 us -> 2.63 us
    psum x3 -> x0, waiting for transfers between devices: 143 us -> none  [on_device(): model = lax.psum(adjoint_product(rows, wave), 'panel')]
    psum x1 -> x0, blocking collectives: 99.4 us -> none  [on_device(): squares = lax.psum(jnp.stack(squares), ('freq', 'panel'))]
    pallas_call x0 -> x1, Pallas kernels: none -> 48.9 us  [solved_spectrum(): pl.pallas_call(functools.partial(lsqr_kernel, panels, blocks), out_shape=...]
    all_to_all x2 -> x1, blocking collectives: 52.3 us -> 22.8 us  [exchange(): lax.all_to_all(lines.reshape(-1), 'freq', split_axis=0, concat_axis=0, ti...]
    all_to_all x0 -> x1, starting transfers between devices: none -> 18.4 us  [exchange(): lax.all_to_all(lines.reshape(-1), 'freq', split_axis=0, concat_axis=0, ti...]
    all_to_all x0 -> x1, waiting for transfers between devices: none -> 9.81 us  [exchange(): lax.all_to_all(lines.reshape(-1), 'freq', split_axis=0, concat_axis=0, ti...]
    dot_general x12 -> x0, matrix products: 6.58 us -> none  [the longest x6 3.43 us: product_of(): both = jnp.dot(rows, right, preferred_element_type=jnp.float32)]
    reduce_sum x7 -> x1, other arithmetic: 5.58 us -> 1.61 us  [on_device(): square = jnp.full((1, 128), jnp.sum(data * data))]
  transfers between devices with their start and end apart: 3 -> 1, of which waited for: 3 -> 1; matrix products, arithmetic and copies ran while one was open for 1% -> 1% of each run, Pallas kernels for 0% -> 0%
where the time goes in v2:
time: 112 us
  Pallas kernels  48.9 us (44%)
  blocking collectives  22.8 us (20%)
  starting transfers between devices  18.4 us (16%)
  waiting for transfers between devices  9.81 us (9%)
  local copies, waits for them, and re-layouts  5.11 us (5%)
  other arithmetic  4.21 us (4%)
  matrix products  2.63 us (2%)
    pallas_call x1, Pallas kernels, solved_spectrum(): pl.pallas_call(functools.partial(lsqr_kernel, panels, blocks), out_shape=...  48.9 us
    all_to_all x1, blocking collectives, exchange(): lax.all_to_all(lines.reshape(-1), 'freq', split_axis=0, concat_axis=0, ti...  22.8 us
    all_to_all x1, starting transfers between devices, exchange(): lax.all_to_all(lines.reshape(-1), 'freq', split_axis=0, concat_axis=0, ti...  18.4 us
    all_to_all x1, waiting for transfers between devices, exchange(): lax.all_to_all(lines.reshape(-1), 'freq', split_axis=0, concat_axis=0, ti...  9.81 us
    unnamed x5, local copies, waits for them, and re-layouts  2.55 us
  transfers between devices with their start and end apart: 1, of which 1 were waited for; matrix products, arithmetic and copies ran while one was open for 1% of the time, Pallas kernels for 0%

profile of v2, /device:TPU:1, one launch (start us, length us, event | category | flops | bytes accessed | tf_op | source)
XLA Modules:
  0.0 112.0 jit_solution(4009940035561107374)
XLA Ops:
  0.0 1.1 cosine_multiply_fusion
  1.1 1.5 %fusion = bf16[128,2,50]{0,2,1:T(8,128)(2,1)S(1)} fusion(f32[1,128,512]{2,1,0:T(8,128)S(1)} %get-tuple-element.6, f32[1,128,512]{2,1,0:T(8,128)S(1)} %get-tuple-element.5, f32[1,50,512]{2,0,1:T(1,128)} %param.3), kind=kOutput, calls=%fused_computation.2 | convolution fusion | flops 78787072 | bytes 652288 | tf_op jit(solution)/shard_map/cft,rt->fcr/dot_general | solution.py:294
  2.6 0.8 copy.5
  3.4 18.4 %all-to-all-start = ((bf16[128,100,1]{1,2,0:T(2,128)(2,1)}), bf16[128,100,1]{1,2,0:T(2,128)(2,1)S(1)}, u32[]{:S(2)}, u32[]{:S(2)}) async-start(bf16[128,100,1]{1,2,0:T(2,128)(2,1)} %copy.5), calls=%async_computation | async-start | bytes 131072 | tf_op jit(solution)/shard_map/all_to_all | solution.py:291
  21.8 1.6 %fusion.7 = f32[]{:T(128)} fusion(f32[1,50,512]{2,0,1:T(1,128)} %param.3), kind=kLoop, calls=%fused_computation.16 | loop fusion | flops 51199 | bytes 102404 | tf_op jit(solution)/shard_map/reduce_sum | solution.py:296
  23.4 9.8 %all-to-all-done = bf16[128,100,1]{1,2,0:T(2,128)(2,1)S(1)} async-done(((bf16[128,100,1]{1,2,0:T(2,128)(2,1)}), bf16[128,100,1]{1,2,0:T(2,128)(2,1)S(1)}, u32[]{:S(2)}, u32[]{:S(2)}) %all-to-all-start) | async-done | bytes 25632 | tf_op jit(solution)/shard_map/all_to_all | solution.py:291
  33.2 0.1 copy.6
  33.4 0.1 copy.7
  33.5 0.1 reshape.114.lines_ref
  33.6 0.7 broadcast_in_dim.3.square_ref
  34.3 0.0 copy-start
  34.3 1.7 %copy-done = bf16[2,1,400,1600]{3,2,1,0:T(8,128)(2,1)S(1)} copy-done((bf16[2,1,400,1600]{3,2,1,0:T(8,128)(2,1)S(1)}, bf16[2,1,400,1600]{3,2,1,0:T(8,128)(2,1)}, u32[]{:S(2)}) %copy-start) | copy-done | bytes 2560024
  36.1 48.9 %shard_map.28 = bf16[32,1600]{1,0:T(8,128)(2,1)S(1)} custom-call(bf16[32,400]{1,0:T(8,128)(2,1)S(1)} %reshape.114.lines_ref, bf16[2,400,1600]{2,1,0:T(8,128)(2,1)S(1)} %bitcast.23, f32[1,128]{1,0:T(1,128)S(1)} %broadcast_in_dim.3.square_ref), custom_call_target="tpu_custom_call" | custom-call | tf_op jit(solution)/shard_map/pallas_call | solution.py:252
  85.0 0.2 reshape.115
  85.2 0.1 copy.8
  85.3 0.2 copy.9
  85.5 0.5 broadcast.119
  86.0 1.5 %reduce = bf16[128,400]{1,0:T(8,128)(2,1)S(1)} reduce(bf16[128,1,400]{2,1,0:T(2,128)(2,1)S(1)} %bitcast.24, bf16[]{:T(256)} %broadcast.119), dimensions={1}, to_apply=%bitcast.20.reduce_sub_computation | reduce | bytes 204802
  87.5 0.1 reshape.120
  87.7 22.8 %all_to_all.18 = bf16[128,2,200]{2,1,0:T(2,128)(2,1)S(1)} all-to-all(bf16[128,2,200]{2,1,0:T(2,128)(2,1)S(1)} %reshape.120), channel_id=1, replica_groups=mesh['freq'=128,'panel'=4] {'freq'}, dimensions={0} | all-to-all | bytes 204800 | tf_op jit(solution)/shard_map/all_to_all | solution.py:291
  110.5 0.2 reshape.121
  110.6 0.2 copy.10
  110.8 1.1 %convolution_bitcast_fusion = f32[200,512]{1,0:T(8,128)} fusion(bf16[128,2,200]{0,2,1:T(8,128)(2,1)S(1)} %bitcast.28, f32[1,128,512]{2,1,0:T(8,128)S(1)} %get-tuple-element.6, f32[1,128,512]{2,1,0:T(8,128)S(1)} %get-tuple-element.5), kind=kOutput, calls=%fused_computation | convolution fusion | flops 314703872 | bytes 1036288 | tf_op jit(solution)/shard_map/jcr,cjt->rt/dot_general | solution.py:299
  (3 shorter events, 0.0 us)
Async XLA Ops:
  3.4 29.8 %all-to-all-start = ((bf16[128,100,1]{1,2,0:T(2,128)(2,1)}), bf16[128,100,1]{1,2,0:T(2,128)(2,1)S(1)}, u32[]{:S(2)}, u32[]{:S(2)}) async-start(bf16[128,100,1]{1,2,0:T(2,128)(2,1)} %copy.5), calls=%async_computation | async-start | bytes 131072 | tf_op jit(solution)/shard_map/all_to_all | solution.py:291
  34.3 1.8 %copy-start = (bf16[2,1,400,1600]{3,2,1,0:T(8,128)(2,1)S(1)}, bf16[2,1,400,1600]{3,2,1,0:T(8,128)(2,1)}, u32[]{:S(2)}) copy-start(bf16[2,1,400,1600]{3,2,1,0:T(8,128)(2,1)} %param.2) | copy-start | bytes 7680004

commit v3 on v2

--- a/solution.py
+++ b/solution.py
@@ -13,6 +13,7 @@
 SCALE = 0.5
 NEAR = 16
 GROUP = 8
+LANES = 128
 MESH = pl.DeviceIdType.MESH
 
 precise = lax.Precision.HIGHEST
@@ -122,6 +123,10 @@
     wave_ref,
     square_ref,
     spectrum_ref,
+    lines_in,
+    data_rows,
+    leaving,
+    landed,
     parts,
     arrived,
     bases,
@@ -129,6 +134,10 @@
     near,
     far,
     across,
+    lines_send,
+    lines_recv,
+    trace_send,
+    trace_recv,
     part_send,
     part_recv,
     base_send,
@@ -150,8 +159,21 @@
     far_peers = [{"freq": (outer + k) % distant * NEAR + inner} for k in range(1, distant)]
 
     barrier = pltpu.get_barrier_semaphore()
-    for peer in panel_peers + near_peers + far_peers:
+    for peer in panel_peers:
         pl.semaphore_signal(barrier, inc=1, device_id=peer, device_id_type=MESH)
+
+    @pl.loop(1, blocks)
+    def _(k):
+        peer = {"freq": (freq + k) % blocks}
+        pl.semaphore_signal(barrier, inc=1, device_id=peer, device_id_type=MESH)
+
+    strips = blocks // VS
+    chunk = bases.shape[-1] // strips
+    half = leaving.shape[-1] // 2
+    span = data_rows.shape[-1] // strips
+
+    def slot_of(index):
+        return index % strips * VS + index // strips
 
     sent = []
 
@@ -170,9 +192,56 @@
     def arrival(ref, recv_sem):
         pltpu.make_async_copy(ref, ref, recv_sem).wait()
 
+    def exchange(source, source_slot, target, target_slot, send_sem, recv_sem):
+        target[target_slot(freq)] = source[source_slot(freq)]
+
+        @pl.loop(1, blocks)
+        def _(k):
+            peer = (freq + k) % blocks
+            pltpu.make_async_remote_copy(
+                src_ref=source.at[source_slot(peer)],
+                dst_ref=target.at[target_slot(freq)],
+                send_sem=send_sem,
+                recv_sem=recv_sem,
+                device_id={"freq": peer},
+                device_id_type=MESH,
+            ).start()
+
+    def exchanged(ref, sem):
+        others = ref.at[pl.ds(0, blocks - 1)]
+        pltpu.make_async_copy(others, others, sem).wait()
+
+    def same(index):
+        return index
+
+    def send_traces(step):
+        model = bases[step].reshape(2 * VS, -1)
+        for strip in range(strips):
+            columns = slice(strip * chunk, (strip + 1) * chunk)
+            slots = slice(strip * VS, (strip + 1) * VS)
+            leaving[step, slots, 0, :chunk] = model[:VS, columns]
+            leaving[step, slots, 0, half : half + chunk] = model[VS:, columns]
+        exchange(
+            leaving.at[step],
+            slot_of,
+            landed.at[step],
+            same,
+            trace_send.at[step],
+            trace_recv.at[step],
+        )
+
+    leaving[...] = jnp.zeros_like(leaving)
     sums[...] = jnp.zeros_like(sums)
     sums[0:1, :] = square_ref[...]
-    rows = lines_ref[...]
+    pl.semaphore_wait(barrier, len(panel_peers) + blocks - 1)
+    exchange(lines_ref, same, lines_in, slot_of, lines_send, lines_recv)
+    exchanged(lines_in, lines_recv)
+    for strip in range(strips):
+        columns = slice(strip * span, (strip + 1) * span)
+        slots = slice(strip * VS, (strip + 1) * VS)
+        data_rows[:VS, columns] = lines_in[slots, 0, :span]
+        data_rows[VS:, columns] = lines_in[slots, 0, LANES // 2 : LANES // 2 + span]
+    rows = two_parts(data_rows[...])
     for step in range(ITERS):
         by_real = product_of(rows, wave_ref[0], 0)
         by_imag = product_of(rows, wave_ref[1], 0)
@@ -180,8 +249,6 @@
         imag_part = SCALE * (by_real[VS:] - by_imag[:VS])
         parts[step, : panels // 2] = real_part.reshape(panels // 2, GROUP, -1)
         parts[step, panels // 2 :] = imag_part.reshape(panels // 2, GROUP, -1)
-        if step == 0:
-            pl.semaphore_wait(barrier, len(panel_peers + near_peers + far_peers))
         for k in range(1, panels):
             copy_to(
                 panel_peers[k - 1],
@@ -190,6 +257,8 @@
                 part_send.at[step, k - 1],
                 part_recv.at[step, k - 1],
             )
+        if step > 0:
+            send_traces(step - 1)
         total = parts[step, me]
         for k in range(1, panels):
             arrival(arrived.at[step, k - 1], part_recv.at[step, k - 1])
@@ -216,7 +285,7 @@
         if step < ITERS - 1:
             rows = two_parts(image)
 
-    def summed(value, held, count, index, peers, send_sem, recv_sem):
+    def summed(value, held, count, index, peers, send_sem, recv_sem, meanwhile=None):
         held[index] = value
         for k in range(1, count):
             copy_to(
@@ -226,35 +295,55 @@
                 send_sem.at[k - 1],
                 recv_sem.at[k - 1],
             )
+        if meanwhile is not None:
+            meanwhile()
         for k in range(1, count):
             arrival(held.at[(index + count - k) % count], recv_sem.at[k - 1])
         return jnp.sum(held[...], axis=0)
 
-    value = summed(sums[...], near, NEAR, inner, near_peers, near_send, near_recv)
+    value = summed(
+        sums[...],
+        near,
+        NEAR,
+        inner,
+        near_peers,
+        near_send,
+        near_recv,
+        lambda: send_traces(ITERS - 1),
+    )
     value = summed(value, far, distant, outer, far_peers, far_send, far_recv)
     value = summed(value, across, panels, me, panel_peers, across_send, across_recv)
     squares = [value[k : k + 1, :] for k in range(2 * ITERS + 1)]
     weights = iterate_weights(squares[0], squares[1:])
-    spectrum = sum(
-        weight[:, :1] * bases[step].reshape(2 * VS, -1) for step, weight in enumerate(weights)
+    for step in range(ITERS):
+        exchanged(landed.at[step], trace_recv.at[step])
+    spectrum_ref[...] = sum(
+        weight[:, :1].reshape(1, 1, 1) * landed[step] for step, weight in enumerate(weights)
     )
-    spectrum_ref[...] = spectrum.astype(jnp.bfloat16)
     for copy in sent:
         copy.wait_send()
-
-
-def solved_spectrum(lines, wave, square, panels, blocks):
+    exchanged(lines_in, lines_send)
+    for step in range(ITERS):
+        exchanged(landed.at[step], trace_send.at[step])
+
+
+def solved_spectra(lines, wave, square, panels, blocks):
     sources = wave.shape[2]
     quarter = (GROUP, sources)
-    tile = (8, 128)
+    tile = (8, LANES)
     distant = blocks // NEAR
+    half = -(-2 * VS * sources // (2 * blocks) // LANES) * LANES
     dma = pltpu.SemaphoreType.DMA
     return pl.pallas_call(
         functools.partial(lsqr_kernel, panels, blocks),
-        out_shape=jax.ShapeDtypeStruct((2 * VS, sources), jnp.bfloat16),
+        out_shape=jax.ShapeDtypeStruct((blocks, 1, 2 * half), jnp.float32),
         in_specs=[pl.BlockSpec(memory_space=pltpu.VMEM)] * 3,
         out_specs=pl.BlockSpec(memory_space=pltpu.VMEM),
         scratch_shapes=[
+            pltpu.VMEM((blocks, 1, LANES), jnp.float32),
+            pltpu.VMEM((2 * VS, wave.shape[1]), jnp.float32),
+            pltpu.VMEM((ITERS, blocks, 1, 2 * half), jnp.float32),
+            pltpu.VMEM((ITERS, blocks, 1, 2 * half), jnp.float32),
             pltpu.VMEM((ITERS, panels, *quarter), jnp.float32),
             pltpu.VMEM((ITERS, panels - 1, *quarter), jnp.float32),
             pltpu.VMEM((ITERS, panels, *quarter), jnp.float32),
@@ -262,6 +351,10 @@
             pltpu.VMEM((NEAR, *tile), jnp.float32),
             pltpu.VMEM((distant, *tile), jnp.float32),
             pltpu.VMEM((panels, *tile), jnp.float32),
+            dma,
+            dma,
+            dma((ITERS,)),
+            dma((ITERS,)),
             dma((ITERS, panels - 1)),
             dma((ITERS, panels - 1)),
             dma((ITERS, panels - 1)),
@@ -281,22 +374,17 @@
 
 def on_device(wave, observed):
     wave = wave[:, 0]
-    panel_rows = wave.shape[1]
     blocks = lax.axis_size("freq")
     panels = lax.axis_size("panel")
     table = transform_tables(blocks, observed.shape[2])
     data = observed[0]
 
-    def exchange(lines):
-        moved = lax.all_to_all(lines.reshape(-1), "freq", split_axis=0, concat_axis=0, tiled=True)
-        return moved.reshape(blocks, 2, -1)
-
-    lines = jnp.einsum("cft,rt->fcr", table, data, precision=precise).astype(jnp.bfloat16)
-    rows = exchange(lines).transpose(1, 0, 2).reshape(2 * VS, panel_rows)
-    square = jnp.full((1, 128), jnp.sum(data * data))
-    spectrum = solved_spectrum(rows, wave, square, panels, blocks).reshape(2, blocks, -1)
-    moved = exchange(spectrum.transpose(1, 0, 2))
-    return jnp.einsum("jcr,cjt->rt", moved.astype(jnp.float32), table, precision=precise)
+    lines = jnp.einsum("cft,rt->fcr", table, data, precision=precise)
+    lines = jnp.pad(lines, ((0, 0), (0, 0), (0, LANES // 2 - data.shape[0])))
+    square = jnp.full((1, LANES), jnp.sum(data * data))
+    spectra = solved_spectra(lines.reshape(blocks, 1, LANES), wave, square, panels, blocks)
+    spectra = spectra.reshape(blocks, 2, -1)[:, :, : VS * wave.shape[2] // blocks]
+    return jnp.einsum("jcr,cjt->rt", spectra, table, precision=precise)
 
 
 def solution(mesh):

time: 112 us -> 82 us (0.73)
  Pallas kernels: 48.9 us -> 73.7 us
  blocking collectives: 22.8 us -> 0 us
  starting transfers between devices: 18.4 us -> 0 us
  waiting for transfers between devices: 9.81 us -> 0 us
  local copies, waits for them, and re-layouts: 5.11 us -> 2.62 us
  other arithmetic: 4.21 us -> 2.64 us
    pallas_call x1, Pallas kernels: 48.9 us -> 73.7 us  [solved_spectra(): pl.pallas_call(functools.partial(lsqr_kernel, panels, blocks), out_shape=...]
    all_to_all x1 -> x0, blocking collectives: 22.8 us -> none  [exchange(): lax.all_to_all(lines.reshape(-1), 'freq', split_axis=0, concat_axis=0, ti...]
    all_to_all x1 -> x0, starting transfers between devices: 18.4 us -> none  [exchange(): lax.all_to_all(lines.reshape(-1), 'freq', split_axis=0, concat_axis=0, ti...]
    all_to_all x1 -> x0, waiting for transfers between devices: 9.81 us -> none  [exchange(): lax.all_to_all(lines.reshape(-1), 'freq', split_axis=0, concat_axis=0, ti...]
    unnamed x1 -> x0, other arithmetic: 1.48 us -> none
    all_to_all x5 -> x0, local copies, waits for them, and re-layouts: 1.26 us -> none  [exchange(): lax.all_to_all(lines.reshape(-1), 'freq', split_axis=0, concat_axis=0, ti...]
    unnamed x5 -> x2, local copies, waits for them, and re-layouts: 2.55 us -> 1.75 us
  transfers between devices with their start and end apart: 1 -> 0, of which waited for: 1 -> 0; matrix products, arithmetic and copies ran while one was open for 1% -> 0% of each run, Pallas kernels for 0% -> 0%
where the time goes in v3:
time: 82 us; the launch traced here: 81.8 us
  Pallas kernels  73.7 us (90%)
  matrix products  2.78 us (3%)
  other arithmetic  2.64 us (3%)
  local copies, waits for them, and re-layouts  2.62 us (3%)
    pallas_call x1, Pallas kernels, solved_spectra(): pl.pallas_call(functools.partial(lsqr_kernel, panels, blocks), out_shape=...  73.7 us
    unnamed x2, local copies, waits for them, and re-layouts  1.75 us

profile of v3, /device:TPU:1, one launch (start us, length us, event | category | flops | bytes accessed | tf_op | source)
XLA Modules:
  0.0 81.8 jit_solution(11593678370815634511)
XLA Ops:
  0.0 1.5 %fusion.7 = f32[]{:T(128)} fusion(f32[1,50,512]{2,0,1:T(1,128)} %param.3), kind=kLoop, calls=%fused_computation.16 | loop fusion | flops 51199 | bytes 102404 | tf_op jit(solution)/shard_map/reduce_sum | solution.py:384
  1.5 0.6 broadcast_in_dim.3.square_ref
  2.2 1.1 %cosine_multiply_fusion = (f32[1,128,512]{2,1,0:T(8,128)S(1)}, f32[1,128,512]{2,1,0:T(8,128)S(1)}) fusion(s32[128]{0:T(128)S(1)} %iota_add_fusion), kind=kLoop, calls=%fused_computation.10 | loop fusion | flops 1048576 | bytes 524800 | tf_op jit(solution)/shard_map/mul | solution.py:28
  3.3 1.5 %convolution_bitcast_fusion.1 = f32[128,2,50]{0,2,1:T(8,128)S(1)} fusion(f32[1,128,512]{2,1,0:T(8,128)S(1)} %get-tuple-element.6, f32[1,128,512]{2,1,0:T(8,128)S(1)} %get-tuple-element.5, f32[1,50,512]{2,0,1:T(1,128)} %param.3), kind=kOutput, calls=%fused_computation.1 | convolution fusion | flops 78774272 | bytes 677888 | tf_op jit(solution)/shard_map/cft,rt->fcr/dot_general | solution.py:382
  4.8 0.1 copy.5.lines_ref
  4.9 0.0 copy-start
  4.9 1.7 %copy-done = bf16[2,1,400,1600]{3,2,1,0:T(8,128)(2,1)S(1)} copy-done((bf16[2,1,400,1600]{3,2,1,0:T(8,128)(2,1)S(1)}, bf16[2,1,400,1600]{3,2,1,0:T(8,128)(2,1)}, u32[]{:S(2)}) %copy-start) | copy-done | bytes 2560024
  6.7 73.7 %shard_map.28 = f32[128,1,512]{2,1,0:T(1,128)S(1)} custom-call(f32[128,1,128]{2,1,0:T(1,128)S(1)} %copy.5.lines_ref, bf16[2,400,1600]{2,1,0:T(8,128)(2,1)S(1)} %bitcast.14, f32[1,128]{1,0:T(1,128)S(1)} %broadcast_in_dim.3.square_ref), custom_call_target="tpu_custom_call" | custom-call | tf_op jit(solution)/shard_map/pallas_call | solution.py:337
  80.4 0.1 copy.7
  80.5 1.3 %convolution_bitcast_fusion = f32[200,512]{1,0:T(8,128)} fusion(f32[1,128,512]{2,1,0:T(8,128)S(1)} %get-tuple-element.6, f32[1,128,512]{2,1,0:T(8,128)S(1)} %get-tuple-element.5, f32[128,2,256]{0,2,1:T(8,128)S(1)} %bitcast.15), kind=kOutput, calls=%fused_computation | convolution fusion | flops 314703872 | bytes 1138688 | tf_op jit(solution)/shard_map/jcr,cjt->rt/dot_general | solution.py:387
  (2 shorter events, 0.0 us)
Async XLA Ops:
  4.9 1.8 %copy-start = (bf16[2,1,400,1600]{3,2,1,0:T(8,128)(2,1)S(1)}, bf16[2,1,400,1600]{3,2,1,0:T(8,128)(2,1)}, u32[]{:S(2)}) copy-start(bf16[2,1,400,1600]{3,2,1,0:T(8,128)(2,1)} %param.2) | copy-start | bytes 7680004

commit v4 on v3

--- a/solution.py
+++ b/solution.py
@@ -3,6 +3,7 @@
 
 import jax
 import jax.numpy as jnp
+import numpy as np
 from jax import lax
 from jax.experimental import pallas as pl
 from jax.experimental.pallas import tpu as pltpu
@@ -11,7 +12,6 @@
 VS = 16
 ITERS = 3
 SCALE = 0.5
-NEAR = 16
 GROUP = 8
 LANES = 128
 MESH = pl.DeviceIdType.MESH
@@ -21,11 +21,11 @@
 
 
 def transform_tables(freq_total, samples):
-    freq_index = lax.broadcasted_iota(jnp.int32, (freq_total, samples), 0) + 1
-    time_index = lax.broadcasted_iota(jnp.int32, (freq_total, samples), 1)
-    phases = (freq_index * time_index % samples).astype(jnp.float32) * (2.0 * math.pi / samples)
+    freq_index = np.arange(freq_total)[:, None] + 1
+    time_index = np.arange(samples)[None, :]
+    phases = (freq_index * time_index % samples) * (2.0 * math.pi / samples)
     factor = math.sqrt(2.0 / samples)
-    return jnp.stack([factor * jnp.cos(phases), -factor * jnp.sin(phases)])
+    return np.stack([factor * np.cos(phases), -factor * np.sin(phases)]).astype(np.float32)
 
 
 def two_parts(field):
@@ -119,10 +119,14 @@
 def lsqr_kernel(
     panels,
     blocks,
-    lines_ref,
+    data_hbm,
+    table_hbm,
+    wave_hbm,
+    spectrum_ref,
+    data_ref,
+    table_ref,
     wave_ref,
-    square_ref,
-    spectrum_ref,
+    lines_out,
     lines_in,
     data_rows,
     leaving,
@@ -130,10 +134,10 @@
     parts,
     arrived,
     bases,
-    sums,
-    near,
-    far,
+    sums_out,
+    sums_in,
     across,
+    load_sem,
     lines_send,
     lines_recv,
     trace_send,
@@ -142,21 +146,22 @@
     part_recv,
     base_send,
     base_recv,
-    near_send,
-    near_recv,
-    far_send,
-    far_recv,
+    sums_send,
+    sums_recv,
     across_send,
     across_recv,
 ):
     me = lax.axis_index("panel")
     freq = lax.axis_index("freq")
-    outer, inner = freq // NEAR, freq % NEAR
-    distant = blocks // NEAR
-
     panel_peers = [{"panel": (me + k) % panels} for k in range(1, panels)]
-    near_peers = [{"freq": outer * NEAR + (inner + k) % NEAR} for k in range(1, NEAR)]
-    far_peers = [{"freq": (outer + k) % distant * NEAR + inner} for k in range(1, distant)]
+
+    loads = [
+        pltpu.make_async_copy(data_hbm, data_ref, load_sem.at[0]),
+        pltpu.make_async_copy(table_hbm, table_ref, load_sem.at[1]),
+        pltpu.make_async_copy(wave_hbm.at[:, 0], wave_ref, load_sem.at[2]),
+    ]
+    for load in loads:
+        load.start()
 
     barrier = pltpu.get_barrier_semaphore()
     for peer in panel_peers:
@@ -230,11 +235,21 @@
             trace_recv.at[step],
         )
 
+    lanes = lax.broadcasted_iota(jnp.int32, (1, LANES), 1)
+    lines_out[...] = jnp.zeros_like(lines_out)
+    loads[0].wait()
+    loads[1].wait()
+    data = data_ref[:, 0, :]
+    squares = [square_of(data)]
+    for part in range(2):
+        first = part * (LANES // 2)
+        lines_out[:, 0, first : first + data.shape[0]] = lax.dot_general(
+            table_ref[part], data, (((1,), (1,)), ((), ())), precision=precise
+        )
+    pl.semaphore_wait(barrier, len(panel_peers) + blocks - 1)
+    exchange(lines_out, same, lines_in, slot_of, lines_send, lines_recv)
     leaving[...] = jnp.zeros_like(leaving)
-    sums[...] = jnp.zeros_like(sums)
-    sums[0:1, :] = square_ref[...]
-    pl.semaphore_wait(barrier, len(panel_peers) + blocks - 1)
-    exchange(lines_ref, same, lines_in, slot_of, lines_send, lines_recv)
+    loads[2].wait()
     exchanged(lines_in, lines_recv)
     for strip in range(strips):
         columns = slice(strip * span, (strip + 1) * span)
@@ -272,7 +287,7 @@
                 base_send.at[step, k - 1],
                 base_recv.at[step, k - 1],
             )
-        sums[2 * step + 1 : 2 * step + 2, :] = square_of(total)
+        squares.append(square_of(total))
         for k in range(1, panels):
             arrival(bases.at[step, (me + panels - k) % panels], base_recv.at[step, k - 1])
         model_rows = two_parts(bases[step].reshape(2 * VS, -1))
@@ -281,76 +296,78 @@
         image = SCALE * jnp.concatenate(
             [by_real[:VS] - by_imag[VS:], by_imag[:VS] + by_real[VS:]]
         )
-        sums[2 * step + 2 : 2 * step + 3, :] = square_of(image)
+        squares.append(square_of(image))
         if step < ITERS - 1:
             rows = two_parts(image)
 
-    def summed(value, held, count, index, peers, send_sem, recv_sem, meanwhile=None):
-        held[index] = value
-        for k in range(1, count):
-            copy_to(
-                peers[k - 1],
-                held.at[index],
-                held.at[index],
-                send_sem.at[k - 1],
-                recv_sem.at[k - 1],
-            )
-        if meanwhile is not None:
-            meanwhile()
-        for k in range(1, count):
-            arrival(held.at[(index + count - k) % count], recv_sem.at[k - 1])
-        return jnp.sum(held[...], axis=0)
-
-    value = summed(
-        sums[...],
-        near,
-        NEAR,
-        inner,
-        near_peers,
-        near_send,
-        near_recv,
-        lambda: send_traces(ITERS - 1),
+    sums_out[0] = sum(
+        jnp.where(lanes == k, square, 0.0) for k, square in enumerate(squares)
     )
-    value = summed(value, far, distant, outer, far_peers, far_send, far_recv)
-    value = summed(value, across, panels, me, panel_peers, across_send, across_recv)
-    squares = [value[k : k + 1, :] for k in range(2 * ITERS + 1)]
+    exchange(sums_out, lambda index: 0, sums_in, same, sums_send, sums_recv)
+    send_traces(ITERS - 1)
+    exchanged(sums_in, sums_recv)
+    across[me] = jnp.sum(sums_in[...], axis=0)
+    for k in range(1, panels):
+        copy_to(
+            panel_peers[k - 1],
+            across.at[me],
+            across.at[me],
+            across_send.at[k - 1],
+            across_recv.at[k - 1],
+        )
+    for k in range(1, panels):
+        arrival(across.at[(me + panels - k) % panels], across_recv.at[k - 1])
+    total = across[0]
+    for k in range(1, panels):
+        total = total + across[k]
+    squares = [
+        jnp.broadcast_to(jnp.sum(jnp.where(lanes == k, total, 0.0), keepdims=True), (1, LANES))
+        for k in range(len(squares))
+    ]
     weights = iterate_weights(squares[0], squares[1:])
+    weights = [jnp.concatenate([weight] * (2 * half // LANES), axis=1) for weight in weights]
     for step in range(ITERS):
         exchanged(landed.at[step], trace_recv.at[step])
-    spectrum_ref[...] = sum(
-        weight[:, :1].reshape(1, 1, 1) * landed[step] for step, weight in enumerate(weights)
-    )
+    for first in range(0, blocks, VS):
+        rows = slice(first, first + VS)
+        spectrum_ref[rows] = sum(
+            weight[None] * landed[step, rows] for step, weight in enumerate(weights)
+        )
     for copy in sent:
         copy.wait_send()
     exchanged(lines_in, lines_send)
+    exchanged(sums_in, sums_send)
     for step in range(ITERS):
         exchanged(landed.at[step], trace_send.at[step])
 
 
-def solved_spectra(lines, wave, square, panels, blocks):
-    sources = wave.shape[2]
+def solved_spectra(data, table, wave, panels, blocks):
+    sources = wave.shape[3]
     quarter = (GROUP, sources)
-    tile = (8, LANES)
-    distant = blocks // NEAR
+    row = (1, LANES)
     half = -(-2 * VS * sources // (2 * blocks) // LANES) * LANES
     dma = pltpu.SemaphoreType.DMA
     return pl.pallas_call(
         functools.partial(lsqr_kernel, panels, blocks),
         out_shape=jax.ShapeDtypeStruct((blocks, 1, 2 * half), jnp.float32),
-        in_specs=[pl.BlockSpec(memory_space=pltpu.VMEM)] * 3,
+        in_specs=[pl.BlockSpec(memory_space=pl.ANY)] * 3,
         out_specs=pl.BlockSpec(memory_space=pltpu.VMEM),
         scratch_shapes=[
-            pltpu.VMEM((blocks, 1, LANES), jnp.float32),
-            pltpu.VMEM((2 * VS, wave.shape[1]), jnp.float32),
+            pltpu.VMEM(data.shape, jnp.float32),
+            pltpu.VMEM(table.shape, jnp.float32),
+            pltpu.VMEM((2, *wave.shape[2:]), jnp.bfloat16),
+            pltpu.VMEM((blocks, *row), jnp.float32),
+            pltpu.VMEM((blocks, *row), jnp.float32),
+            pltpu.VMEM((2 * VS, wave.shape[2]), jnp.float32),
             pltpu.VMEM((ITERS, blocks, 1, 2 * half), jnp.float32),
             pltpu.VMEM((ITERS, blocks, 1, 2 * half), jnp.float32),
             pltpu.VMEM((ITERS, panels, *quarter), jnp.float32),
             pltpu.VMEM((ITERS, panels - 1, *quarter), jnp.float32),
             pltpu.VMEM((ITERS, panels, *quarter), jnp.float32),
-            pltpu.VMEM(tile, jnp.float32),
-            pltpu.VMEM((NEAR, *tile), jnp.float32),
-            pltpu.VMEM((distant, *tile), jnp.float32),
-            pltpu.VMEM((panels, *tile), jnp.float32),
+            pltpu.VMEM((1, *row), jnp.float32),
+            pltpu.VMEM((blocks, *row), jnp.float32),
+            pltpu.VMEM((panels, *row), jnp.float32),
+            dma((3,)),
             dma,
             dma,
             dma((ITERS,)),
@@ -359,31 +376,24 @@
             dma((ITERS, panels - 1)),
             dma((ITERS, panels - 1)),
             dma((ITERS, panels - 1)),
-            dma((NEAR - 1,)),
-            dma((NEAR - 1,)),
-            dma((distant - 1,)),
-            dma((distant - 1,)),
+            dma,
+            dma,
             dma((panels - 1,)),
             dma((panels - 1,)),
         ],
         compiler_params=pltpu.CompilerParams(
-            collective_id=0, has_side_effects=True, vmem_limit_bytes=32 * 1024 * 1024
+            collective_id=0, has_side_effects=True, vmem_limit_bytes=63 * 1024 * 1024
         ),
-    )(lines, wave, square)
+    )(data, table, wave)
 
 
 def on_device(wave, observed):
-    wave = wave[:, 0]
     blocks = lax.axis_size("freq")
     panels = lax.axis_size("panel")
-    table = transform_tables(blocks, observed.shape[2])
-    data = observed[0]
-
-    lines = jnp.einsum("cft,rt->fcr", table, data, precision=precise)
-    lines = jnp.pad(lines, ((0, 0), (0, 0), (0, LANES // 2 - data.shape[0])))
-    square = jnp.full((1, LANES), jnp.sum(data * data))
-    spectra = solved_spectra(lines.reshape(blocks, 1, LANES), wave, square, panels, blocks)
-    spectra = spectra.reshape(blocks, 2, -1)[:, :, : VS * wave.shape[2] // blocks]
+    table = jnp.asarray(transform_tables(blocks, observed.shape[2]))
+    traces = observed.transpose(1, 0, 2)
+    spectra = solved_spectra(traces, table, wave, panels, blocks)
+    spectra = spectra.reshape(blocks, 2, -1)[:, :, : VS * wave.shape[3] // blocks]
     return jnp.einsum("jcr,cjt->rt", spectra, table, precision=precise)
 
 

time: 82 us -> 74.4 us (0.907)
  other arithmetic: 2.64 us -> 0 us
  Pallas kernels: 73.7 us -> 71.8 us
  local copies, waits for them, and re-layouts: 2.62 us -> 1.08 us
  matrix products: 2.78 us -> 1.29 us
    pallas_call x1, Pallas kernels: 73.7 us -> 71.8 us  [solved_spectra(): pl.pallas_call(functools.partial(lsqr_kernel, panels, blocks), out_shape=...]
    unnamed x2, local copies, waits for them, and re-layouts: 1.75 us -> 0.01 us
    reduce_sum x1 -> x0, other arithmetic: 1.53 us -> none  [on_device(): square = jnp.full((1, LANES), jnp.sum(data * data))]
    dot_general x1 -> x0, matrix products: 1.49 us -> none  [on_device(): lines = jnp.einsum('cft,rt->fcr', table, data, precision=precise)]
    mul x1 -> x0, other arithmetic: 1.11 us -> none  [transform_tables(): return jnp.stack([factor * jnp.cos(phases), -factor * jnp.sin(phases)])]
    reshape x2 -> x1, local copies, waits for them, and re-layouts: 0.22 us -> 1.07 us  [on_device(): spectra.reshape(blocks, 2, -1)[:, :, :VS * wave.shape[3] // blocks]]
where the time goes in v4:
time: 74.4 us; the launch traced here: 74.2 us
  Pallas kernels  71.8 us (97%)
  matrix products  1.29 us (2%)
  local copies, waits for them, and re-layouts  1.08 us (1%)
    pallas_call x1, Pallas kernels, solved_spectra(): pl.pallas_call(functools.partial(lsqr_kernel, panels, blocks), out_shape=...  71.8 us

profile of v4, /device:TPU:1, one launch (start us, length us, event | category | flops | bytes accessed | tf_op | source)
XLA Modules:
  0.0 74.2 jit_solution(15608760811636705178)
XLA Ops:
  0.0 0.0 copy-start
  0.0 71.8 %shard_map.37 = f32[128,1,512]{2,1,0:T(1,128)} custom-call(f32[50,1,512]{2,1,0:T(1,128)} %bitcast.6, f32[2,128,512]{2,1,0:T(8,128)} %constant.2.clone.table_hbm, bf16[2,1,400,1600]{3,2,1,0:T(8,128)(2,1)} %wave_hbm.1), custom_call_target="tpu_custom_call" | custom-call | tf_op jit(solution)/shard_map/pallas_call | solution.py:350
  71.9 1.1 %copy.5 = f32[128,1,512]{0,2,1:T(8,128)S(1)} copy(f32[128,1,512]{2,1,0:T(1,128)} %shard_map.37) | data formatting | bytes 524288 | tf_op jit(solution)/shard_map/reshape | solution.py:396
  72.9 0.0 copy-done
  72.9 1.3 %convolution_bitcast_fusion = f32[200,512]{1,0:T(8,128)} fusion(f32[2,128,512]{2,1,0:T(8,128)S(1)} %copy-done, f32[128,2,256]{0,2,1:T(8,128)S(1)} %bitcast.5), kind=kOutput, calls=%fused_computation | convolution fusion | flops 314572800 | bytes 1138688 | tf_op jit(solution)/shard_map/jcr,cjt->rt/dot_general | solution.py:397
Async XLA Ops:
  0.0 72.9 %copy-start = (f32[2,128,512]{2,1,0:T(8,128)S(1)}, f32[2,128,512]{2,1,0:T(8,128)}, u32[]{:S(2)}) copy-start(f32[2,128,512]{2,1,0:T(8,128)} %constant.2.clone.table_hbm) | copy-start | bytes 1572868

commit v5 on v4

--- a/solution.py
+++ b/solution.py
@@ -13,6 +13,7 @@
 ITERS = 3
 SCALE = 0.5
 GROUP = 8
+UNROLL = 8
 LANES = 128
 MESH = pl.DeviceIdType.MESH
 
@@ -134,6 +135,9 @@
     parts,
     arrived,
     bases,
+    parts_short,
+    arrived_short,
+    bases_short,
     sums_out,
     sums_in,
     across,
@@ -167,9 +171,20 @@
     for peer in panel_peers:
         pl.semaphore_signal(barrier, inc=1, device_id=peer, device_id_type=MESH)
 
-    @pl.loop(1, blocks)
+    def for_others(body):
+        groups = (blocks - 1) // UNROLL
+
+        @pl.loop(0, groups)
+        def _(group):
+            for k in range(UNROLL):
+                body(group * UNROLL + k + 1)
+
+        for k in range(groups * UNROLL + 1, blocks):
+            body(k)
+
+    @for_others
     def _(k):
-        peer = {"freq": (freq + k) % blocks}
+        peer = {"freq": lax.rem(freq + k, blocks)}
         pl.semaphore_signal(barrier, inc=1, device_id=peer, device_id_type=MESH)
 
     strips = blocks // VS
@@ -178,7 +193,7 @@
     span = data_rows.shape[-1] // strips
 
     def slot_of(index):
-        return index % strips * VS + index // strips
+        return lax.rem(index, strips) * VS + lax.div(index, strips)
 
     sent = []
 
@@ -200,9 +215,9 @@
     def exchange(source, source_slot, target, target_slot, send_sem, recv_sem):
         target[target_slot(freq)] = source[source_slot(freq)]
 
-        @pl.loop(1, blocks)
+        @for_others
         def _(k):
-            peer = (freq + k) % blocks
+            peer = lax.rem(freq + k, blocks)
             pltpu.make_async_remote_copy(
                 src_ref=source.at[source_slot(peer)],
                 dst_ref=target.at[target_slot(freq)],
@@ -219,8 +234,10 @@
     def same(index):
         return index
 
+    models = []
+
     def send_traces(step):
-        model = bases[step].reshape(2 * VS, -1)
+        model = models[step]
         for strip in range(strips):
             columns = slice(strip * chunk, (strip + 1) * chunk)
             slots = slice(strip * VS, (strip + 1) * VS)
@@ -262,35 +279,43 @@
         by_imag = product_of(rows, wave_ref[1], 0)
         real_part = SCALE * (by_real[:VS] + by_imag[VS:])
         imag_part = SCALE * (by_real[VS:] - by_imag[:VS])
-        parts[step, : panels // 2] = real_part.reshape(panels // 2, GROUP, -1)
-        parts[step, panels // 2 :] = imag_part.reshape(panels // 2, GROUP, -1)
+        short = step != 1
+        place = step // 2
+        out_parts, in_parts, totals = (
+            (parts_short, arrived_short, bases_short) if short else (parts, arrived, bases)
+        )
+        kind = out_parts.dtype
+        out_parts[place, : panels // 2] = real_part.astype(kind).reshape(panels // 2, GROUP, -1)
+        out_parts[place, panels // 2 :] = imag_part.astype(kind).reshape(panels // 2, GROUP, -1)
         for k in range(1, panels):
             copy_to(
                 panel_peers[k - 1],
-                parts.at[step, (me + k) % panels],
-                arrived.at[step, k - 1],
+                out_parts.at[place, (me + k) % panels],
+                in_parts.at[place, k - 1],
                 part_send.at[step, k - 1],
                 part_recv.at[step, k - 1],
             )
         if step > 0:
             send_traces(step - 1)
-        total = parts[step, me]
+        total = out_parts[place, me].astype(jnp.float32)
         for k in range(1, panels):
-            arrival(arrived.at[step, k - 1], part_recv.at[step, k - 1])
-            total = total + arrived[step, k - 1]
-        bases[step, me] = total
+            arrival(in_parts.at[place, k - 1], part_recv.at[step, k - 1])
+            total = total + in_parts[place, k - 1].astype(jnp.float32)
+        totals[place, me] = total.astype(kind)
         for k in range(1, panels):
             copy_to(
                 panel_peers[k - 1],
-                bases.at[step, me],
-                bases.at[step, me],
+                totals.at[place, me],
+                totals.at[place, me],
                 base_send.at[step, k - 1],
                 base_recv.at[step, k - 1],
             )
-        squares.append(square_of(total))
+        squares.append(square_of(totals[place, me].astype(jnp.float32)))
         for k in range(1, panels):
-            arrival(bases.at[step, (me + panels - k) % panels], base_recv.at[step, k - 1])
-        model_rows = two_parts(bases[step].reshape(2 * VS, -1))
+            arrival(totals.at[place, (me + panels - k) % panels], base_recv.at[step, k - 1])
+        model = totals[place].astype(jnp.float32).reshape(2 * VS, -1)
+        models.append(model)
+        model_rows = model.astype(jnp.bfloat16) if short else two_parts(model)
         by_real = product_of(model_rows, wave_ref[0], 1)
         by_imag = product_of(model_rows, wave_ref[1], 1)
         image = SCALE * jnp.concatenate(
@@ -361,9 +386,12 @@
             pltpu.VMEM((2 * VS, wave.shape[2]), jnp.float32),
             pltpu.VMEM((ITERS, blocks, 1, 2 * half), jnp.float32),
             pltpu.VMEM((ITERS, blocks, 1, 2 * half), jnp.float32),
-            pltpu.VMEM((ITERS, panels, *quarter), jnp.float32),
-            pltpu.VMEM((ITERS, panels - 1, *quarter), jnp.float32),
-            pltpu.VMEM((ITERS, panels, *quarter), jnp.float32),
+            pltpu.VMEM((1, panels, *quarter), jnp.float32),
+            pltpu.VMEM((1, panels - 1, *quarter), jnp.float32),
+            pltpu.VMEM((1, panels, *quarter), jnp.float32),
+            pltpu.VMEM((2, panels, *quarter), jnp.bfloat16),
+            pltpu.VMEM((2, panels - 1, *quarter), jnp.bfloat16),
+            pltpu.VMEM((2, panels, *quarter), jnp.bfloat16),
             pltpu.VMEM((1, *row), jnp.float32),
             pltpu.VMEM((blocks, *row), jnp.float32),
             pltpu.VMEM((panels, *row), jnp.float32),

time: 74.4 us -> 69.6 us (0.935)
  Pallas kernels: 71.8 us -> 67.1 us
    pallas_call x1, Pallas kernels: 71.8 us -> 67.1 us  [solved_spectra(): pl.pallas_call(functools.partial(lsqr_kernel, panels, blocks), out_shape=...]
where the time goes in v5:
time: 69.6 us; the launch traced here: 69.5 us
  Pallas kernels  67.1 us (96%)
  matrix products  1.29 us (2%)
  local copies, waits for them, and re-layouts  1.08 us (2%)
    pallas_call x1, Pallas kernels, solved_spectra(): pl.pallas_call(functools.partial(lsqr_kernel, panels, blocks), out_shape=...  67.1 us

profile of v5, /device:TPU:1, one launch (start us, length us, event | category | flops | bytes accessed | tf_op | source)
XLA Modules:
  0.0 69.5 jit_solution(15716571665412755499)
XLA Ops:
  0.0 0.0 copy-start
  0.0 67.1 %shard_map.37 = f32[128,1,512]{2,1,0:T(1,128)} custom-call(f32[50,1,512]{2,1,0:T(1,128)} %bitcast.6, f32[2,128,512]{2,1,0:T(8,128)} %constant.2.clone.table_hbm, bf16[2,1,400,1600]{3,2,1,0:T(8,128)(2,1)} %wave_hbm.1), custom_call_target="tpu_custom_call" | custom-call | tf_op jit(solution)/shard_map/pallas_call | solution.py:375
  67.1 1.1 %copy.5 = f32[128,1,512]{0,2,1:T(8,128)S(1)} copy(f32[128,1,512]{2,1,0:T(1,128)} %shard_map.37) | data formatting | bytes 524288 | tf_op jit(solution)/shard_map/reshape | solution.py:424
  68.2 0.0 copy-done
  68.2 1.3 %convolution_bitcast_fusion = f32[200,512]{1,0:T(8,128)} fusion(f32[2,128,512]{2,1,0:T(8,128)S(1)} %copy-done, f32[128,2,256]{0,2,1:T(8,128)S(1)} %bitcast.5), kind=kOutput, calls=%fused_computation | convolution fusion | flops 314572800 | bytes 1138688 | tf_op jit(solution)/shard_map/jcr,cjt->rt/dot_general | solution.py:425
Async XLA Ops:
  0.0 68.2 %copy-start = (f32[2,128,512]{2,1,0:T(8,128)S(1)}, f32[2,128,512]{2,1,0:T(8,128)}, u32[]{:S(2)}) copy-start(f32[2,128,512]{2,1,0:T(8,128)} %constant.2.clone.table_hbm) | copy-start | bytes 1572868

commit v6 on v5

--- a/solution.py
+++ b/solution.py
@@ -13,7 +13,7 @@
 ITERS = 3
 SCALE = 0.5
 GROUP = 8
-UNROLL = 8
+UNROLL = 7
 LANES = 128
 MESH = pl.DeviceIdType.MESH
 
@@ -157,6 +157,7 @@
 ):
     me = lax.axis_index("panel")
     freq = lax.axis_index("freq")
+    farthest = sorted(range(1, panels), key=lambda k: -min(k, panels - k))
     panel_peers = [{"panel": (me + k) % panels} for k in range(1, panels)]
 
     loads = [
@@ -172,15 +173,22 @@
         pl.semaphore_signal(barrier, inc=1, device_id=peer, device_id_type=MESH)
 
     def for_others(body):
-        groups = (blocks - 1) // UNROLL
+        middle = blocks // 2
+        groups = (middle - 1) // UNROLL
+
+        def pair(step):
+            body(middle + step)
+            body(middle - step)
+
+        body(middle)
 
         @pl.loop(0, groups)
         def _(group):
             for k in range(UNROLL):
-                body(group * UNROLL + k + 1)
-
-        for k in range(groups * UNROLL + 1, blocks):
-            body(k)
+                pair(group * UNROLL + k + 1)
+
+        for k in range(groups * UNROLL + 1, middle):
+            pair(k)
 
     @for_others
     def _(k):
@@ -279,15 +287,15 @@
         by_imag = product_of(rows, wave_ref[1], 0)
         real_part = SCALE * (by_real[:VS] + by_imag[VS:])
         imag_part = SCALE * (by_real[VS:] - by_imag[:VS])
-        short = step != 1
-        place = step // 2
+        short = step == 0
+        place = 0 if short else step - 1
         out_parts, in_parts, totals = (
             (parts_short, arrived_short, bases_short) if short else (parts, arrived, bases)
         )
         kind = out_parts.dtype
         out_parts[place, : panels // 2] = real_part.astype(kind).reshape(panels // 2, GROUP, -1)
         out_parts[place, panels // 2 :] = imag_part.astype(kind).reshape(panels // 2, GROUP, -1)
-        for k in range(1, panels):
+        for k in farthest:
             copy_to(
                 panel_peers[k - 1],
                 out_parts.at[place, (me + k) % panels],
@@ -302,7 +310,7 @@
             arrival(in_parts.at[place, k - 1], part_recv.at[step, k - 1])
             total = total + in_parts[place, k - 1].astype(jnp.float32)
         totals[place, me] = total.astype(kind)
-        for k in range(1, panels):
+        for k in farthest:
             copy_to(
                 panel_peers[k - 1],
                 totals.at[place, me],
@@ -332,7 +340,7 @@
     send_traces(ITERS - 1)
     exchanged(sums_in, sums_recv)
     across[me] = jnp.sum(sums_in[...], axis=0)
-    for k in range(1, panels):
+    for k in farthest:
         copy_to(
             panel_peers[k - 1],
             across.at[me],
@@ -386,12 +394,12 @@
             pltpu.VMEM((2 * VS, wave.shape[2]), jnp.float32),
             pltpu.VMEM((ITERS, blocks, 1, 2 * half), jnp.float32),
             pltpu.VMEM((ITERS, blocks, 1, 2 * half), jnp.float32),
-            pltpu.VMEM((1, panels, *quarter), jnp.float32),
-            pltpu.VMEM((1, panels - 1, *quarter), jnp.float32),
-            pltpu.VMEM((1, panels, *quarter), jnp.float32),
-            pltpu.VMEM((2, panels, *quarter), jnp.bfloat16),
-            pltpu.VMEM((2, panels - 1, *quarter), jnp.bfloat16),
-            pltpu.VMEM((2, panels, *quarter), jnp.bfloat16),
+            pltpu.VMEM((ITERS - 1, panels, *quarter), jnp.float32),
+            pltpu.VMEM((ITERS - 1, panels - 1, *quarter), jnp.float32),
+            pltpu.VMEM((ITERS - 1, panels, *quarter), jnp.float32),
+            pltpu.VMEM((1, panels, *quarter), jnp.bfloat16),
+            pltpu.VMEM((1, panels - 1, *quarter), jnp.bfloat16),
+            pltpu.VMEM((1, panels, *quarter), jnp.bfloat16),
             pltpu.VMEM((1, *row), jnp.float32),
             pltpu.VMEM((blocks, *row), jnp.float32),
             pltpu.VMEM((panels, *row), jnp.float32),

time: 69.6 us -> 70.1 us (level)
  no operation moved by 1% of the time
where the time goes in v6:
time: 70.1 us; the launch traced here: 70 us
  Pallas kernels  67.6 us (96%)
  matrix products  1.29 us (2%)
  local copies, waits for them, and re-layouts  1.08 us (2%)
    pallas_call x1, Pallas kernels, solved_spectra(): pl.pallas_call(functools.partial(lsqr_kernel, panels, blocks), out_shape=...  67.6 us

profile of v6, /device:TPU:1, one launch (start us, length us, event | category | flops | bytes accessed | tf_op | source)
XLA Modules:
  0.0 70.0 jit_solution(5779933184080543103)
XLA Ops:
  0.0 0.0 copy-start
  0.0 67.6 %shard_map.37 = f32[128,1,512]{2,1,0:T(1,128)} custom-call(f32[50,1,512]{2,1,0:T(1,128)} %bitcast.6, f32[2,128,512]{2,1,0:T(8,128)} %constant.2.clone.table_hbm, bf16[2,1,400,1600]{3,2,1,0:T(8,128)(2,1)} %wave_hbm.1), custom_call_target="tpu_custom_call" | custom-call | tf_op jit(solution)/shard_map/pallas_call | solution.py:383
  67.6 1.1 %copy.5 = f32[128,1,512]{0,2,1:T(8,128)S(1)} copy(f32[128,1,512]{2,1,0:T(1,128)} %shard_map.37) | data formatting | bytes 524288 | tf_op jit(solution)/shard_map/reshape | solution.py:432
  68.7 0.0 copy-done
  68.7 1.3 %convolution_bitcast_fusion = f32[200,512]{1,0:T(8,128)} fusion(f32[2,128,512]{2,1,0:T(8,128)S(1)} %copy-done, f32[128,2,256]{0,2,1:T(8,128)S(1)} %bitcast.5), kind=kOutput, calls=%fused_computation | convolution fusion | flops 314572800 | bytes 1138688 | tf_op jit(solution)/shard_map/jcr,cjt->rt/dot_general | solution.py:433
Async XLA Ops:
  0.0 68.7 %copy-start = (f32[2,128,512]{2,1,0:T(8,128)S(1)}, f32[2,128,512]{2,1,0:T(8,128)}, u32[]{:S(2)}) copy-start(f32[2,128,512]{2,1,0:T(8,128)} %constant.2.clone.table_hbm) | copy-start | bytes 1572868
